TPU v7x, 256 devices: a whole 4x4x8 slice. The times are simulated.
256 devices in a mesh: sy: 8 (over z), sx: 32 (over y, x, core).
Axes of the slice: x: 4, y: 4, z: 8, core: 2. Of those that a mesh axis runs over, the one named last changes fastest.
Arguments:
- sky_image: float32 [2048, 4096], P('sy', 'sx'), may hold values from -6 to 6
- observed: float32 [2048, 4096], P('sy', 'sx'), may hold values from -6 to 6
- noise_weight: float32 [2048, 4096], P('sy', 'sx'), may hold values from 0.25 to 4
- basis_tiles: bfloat16 [1024, 128, 128], P(('sy', 'sx')), may hold values from -3 to 3
- intersection: int32 [16, 32, 4], replicated, may hold values from 0 to 1023, as said below
- counts: int32 [16, 32], P('sy', 'sx'), may hold values from 1 to 4
- transfer: float32 [4, 2, 2048, 4096], P(None, None, ('sy', 'sx')), may hold values from -6 to 6
Outputs:
- residual: float32 [2048, 4096], P('sy', 'sx')
- gradient: float32 [2048, 4096], P('sy', 'sx')
Inputs may be any that keep to these rules, and one draw needn't show every extreme that they name: `intersection`: every entry names a basis tile held by a device with the same sy index as the sky tile. Of the 8 entries of one device's sky tiles, at most 2 name tiles held by any one device, and in every draw each device reaches 2 at one holder.
All inputs are finite; a program needn't handle non-finite values.
Results may differ from a plain program's by a relative error of at most 0.00045.
Values may be sent and summed in bfloat16 or wider, within the bound.
No kernel may reach another device: no remote copies, remote signals or barrier semaphores. Data moves between devices by JAX's collectives and lax.ppermute only.
A program may use at most 128 MiB of HBM per device.

v0:
```python
import jax
import jax.numpy as jnp
from jax import lax
from jax.sharding import PartitionSpec as P

radix = 128
highest = lax.Precision.HIGHEST
tv_weight = 0.5
smoothing = 0.25


def with_halo(block, sides, width):
    for axis, dim in sides:
        count = lax.axis_size(axis)
        forward = [(i, i + 1) for i in range(count - 1)]
        forward.append((count - 1, 0))
        backward = [(target, source) for source, target in forward]
        low = lax.ppermute(
            lax.slice_in_dim(block, block.shape[dim] - width, None, axis=dim), axis, forward
        )
        high = lax.ppermute(lax.slice_in_dim(block, 0, width, axis=dim), axis, backward)
        block = jnp.concatenate([low, block, high], axis=dim)
    return block


def circle(left_index, right_index, length, orient):
    product = left_index[:, None] * right_index[None, :] % length
    angles = product.astype(jnp.float32) * (2.0 * jnp.pi / length)
    return (jnp.cos(angles), orient * jnp.sin(angles))


def contract(pattern, operand, matrix):
    return jnp.einsum(pattern, operand, matrix, precision=highest)


def forward_last(stacked):
    num_parts, num_fields, num_lines, length = stacked.shape
    short_size = length // radix
    pieces = stacked.reshape(num_parts, num_fields, num_lines, short_size, radix)
    short_index = jnp.arange(short_size, dtype=jnp.int32)
    long_index = jnp.arange(radix, dtype=jnp.int32)
    cos_short, sin_short = circle(short_index, short_index, short_size, -1.0)
    cos_turn, sin_turn = circle(short_index, long_index, length, -1.0)
    cos_long, sin_long = circle(long_index, long_index, radix, -1.0)
    first_form = "fmba,bk->fmka"
    real_part = contract(first_form, pieces[0], cos_short)
    imag_part = contract(first_form, pieces[0], sin_short)
    if num_parts == 2:
        real_part = real_part - contract(first_form, pieces[1], sin_short)
        imag_part = imag_part + contract(first_form, pieces[1], cos_short)
    turned_real = real_part * cos_turn - imag_part * sin_turn
    turned_imag = real_part * sin_turn + imag_part * cos_turn
    second_form = "fmka,aj->fmkj"
    out_real = contract(second_form, turned_real, cos_long) - contract(
        second_form, turned_imag, sin_long
    )
    out_imag = contract(second_form, turned_real, sin_long) + contract(
        second_form, turned_imag, cos_long
    )
    return jnp.stack([out_real, out_imag]).reshape(2, num_fields, num_lines, length)


def inverse_last(stacked, real_only):
    num_fields, num_lines, length = (stacked.shape[1], stacked.shape[2], stacked.shape[3])
    short_size = length // radix
    pieces = stacked.reshape(2, num_fields, num_lines, short_size, radix)
    short_index = jnp.arange(short_size, dtype=jnp.int32)
    long_index = jnp.arange(radix, dtype=jnp.int32)
    cos_long, sin_long = circle(long_index, long_index, radix, 1.0)
    cos_turn, sin_turn = circle(short_index, long_index, length, 1.0)
    cos_short, sin_short = circle(short_index, short_index, short_size, 1.0)
    first_form = "fmkj,ja->fmka"
    real_part = contract(first_form, pieces[0], cos_long) - contract(
        first_form, pieces[1], sin_long
    )
    imag_part = contract(first_form, pieces[0], sin_long) + contract(
        first_form, pieces[1], cos_long
    )
    turned_real = real_part * cos_turn - imag_part * sin_turn
    turned_imag = real_part * sin_turn + imag_part * cos_turn
    second_form = "fmka,kb->fmba"
    out_real = contract(second_form, turned_real, cos_short) - contract(
        second_form, turned_imag, sin_short
    )
    if real_only:
        return out_real.reshape(1, num_fields, num_lines, length)
    out_imag = contract(second_form, turned_real, sin_short) + contract(
        second_form, turned_imag, cos_short
    )
    return jnp.stack([out_real, out_imag]).reshape(2, num_fields, num_lines, length)


def to_spectra(pixels):
    columns = lax.all_to_all(
        jnp.swapaxes(pixels, 2, 3), "sy", split_axis=2, concat_axis=3, tiled=True
    )
    along_y = forward_last(columns)
    blocks = lax.all_to_all(along_y, "sy", split_axis=3, concat_axis=2, tiled=True)
    lines = lax.all_to_all(
        jnp.swapaxes(blocks, 2, 3), "sx", split_axis=2, concat_axis=3, tiled=True
    )
    return forward_last(lines)


def from_spectra(spectrum, normalizer):
    along_x = inverse_last(spectrum, False)
    blocks = lax.all_to_all(along_x, "sx", split_axis=3, concat_axis=2, tiled=True)
    columns = lax.all_to_all(
        jnp.swapaxes(blocks, 2, 3), "sy", split_axis=2, concat_axis=3, tiled=True
    )
    values = inverse_last(columns, True) * normalizer
    pixel_blocks = lax.all_to_all(values, "sy", split_axis=3, concat_axis=2, tiled=True)
    return jnp.swapaxes(pixel_blocks, 2, 3)[0]


def on_device(sky_image, observed, noise_weight, basis_tiles, intersection, counts, transfer):
    height, breadth = sky_image.shape
    pool_size, tile_side = (basis_tiles.shape[0], basis_tiles.shape[1])
    components = intersection.shape[2]
    tiles_down = height // tile_side
    tiles_across = breadth // tile_side
    band_size = lax.axis_size("sx")
    sky_row = lax.axis_index("sy")
    sky_column = lax.axis_index("sx")
    num_requests = tiles_down * tiles_across * components
    zero_index = jnp.zeros((), jnp.int32)
    own_lists = lax.dynamic_slice(
        intersection,
        (sky_row * tiles_down, sky_column * tiles_across, zero_index),
        (tiles_down, tiles_across, components),
    ).reshape(num_requests)
    band_start = sky_row * band_size * pool_size
    band_index = own_lists - band_start
    flat_tiles = basis_tiles.reshape(pool_size, tile_side * tile_side)
    piece = lax.all_gather(flat_tiles, "sx", axis=0, tiled=True)
    piece_count = piece.shape[0]
    hits = (band_index[:, None] == jnp.arange(piece_count, dtype=jnp.int32)[None, :]).astype(
        jnp.bfloat16
    )
    coefficient = jnp.dot(hits, piece, preferred_element_type=jnp.float32)
    in_use = (jnp.arange(components, dtype=jnp.int32)[None, None, :] < counts[:, :, None]).astype(
        jnp.float32
    )
    coef_maps = (
        coefficient.reshape(tiles_down, tiles_across, components, tile_side, tile_side)
        * in_use[:, :, :, None, None]
    )
    weights = coef_maps.transpose(2, 0, 3, 1, 4).reshape(components, height, breadth)
    normalizer = 1.0 / (transfer.shape[2] * lax.axis_size("sy") * band_size * transfer.shape[3])
    spectra = to_spectra((weights * sky_image[None])[None])
    trans_real = transfer[:, 0]
    trans_imag = transfer[:, 1]
    model_real = jnp.sum(spectra[0] * trans_real - spectra[1] * trans_imag, axis=0)
    model_imag = jnp.sum(spectra[0] * trans_imag + spectra[1] * trans_real, axis=0)
    blurred = from_spectra(jnp.stack([model_real, model_imag])[:, None], normalizer)[0]
    residual = noise_weight * (blurred - observed)
    back_spectrum = to_spectra(residual[None, None])
    pull_real = back_spectrum[0] * trans_real + back_spectrum[1] * trans_imag
    pull_imag = back_spectrum[1] * trans_real - back_spectrum[0] * trans_imag
    pulled = from_spectra(jnp.stack([pull_real, pull_imag]), normalizer)
    data_grad = jnp.sum(weights * pulled, axis=0)
    framed = with_halo(sky_image, (("sy", 0), ("sx", 1)), 1)
    step_x = framed[:-1, 1:] - framed[:-1, :-1]
    step_y = framed[1:, :-1] - framed[:-1, :-1]
    magnitude = jnp.sqrt(step_x * step_x + step_y * step_y + smoothing)
    flow_x = step_x / magnitude
    flow_y = step_y / magnitude
    spread = flow_x[1:, 1:] - flow_x[1:, :-1] + flow_y[1:, 1:] - flow_y[:-1, 1:]
    gradient = data_grad - tv_weight * spread
    return (residual, gradient)


def solution(mesh):
    placed = (
        P("sy", "sx"),
        P("sy", "sx"),
        P("sy", "sx"),
        P(("sy", "sx"), None, None),
        P(),
        P("sy", "sx"),
        P(None, None, ("sy", "sx"), None),
    )
    return jax.shard_map(
        on_device,
        mesh=mesh,
        in_specs=placed,
        out_specs=(P("sy", "sx"), P("sy", "sx")),
        check_vma=False,
    )
```

profile of v0, /device:TPU:1, one launch (start us, length us, event | category | flops | bytes accessed | tf_op | source)
XLA Modules:
  0.0 563.4 jit_solution(1896056630567575980)
XLA Ops:
  10.5 56.0 %all-gather.3.cloned.1.call-done = bf16[32,4,16384]{2,1,0:T(4,128)(2,1)} async-done(((bf16[1,4,16384]{2,1,0:T(4,128)(2,1)}), bf16[32,4,16384]{2,1,0:T(4,128)(2,1)}) %all-gather.3.cloned.1.call-update) | async-done | bytes 4194320 | tf_op jit(solution)/shard_map/all_gather | solution.py:135
  66.5 6.9 %reshape.406 = bf16[128,16384]{1,0:T(8,128)(2,1)} reshape(bf16[32,4,16384]{2,1,0:T(4,128)(2,1)} %all-gather.3.cloned.1.call-done) | data formatting | bytes 8388608
  85.2 17.9 %all-to-all-done = f32[1,4,128,256]{3,1,0,2:T(4,128)S(1)} async-done(((f32[1,4,128,256]{3,1,0,2:T(4,128)}), f32[1,4,128,256]{3,1,0,2:T(4,128)S(1)}, u32[]{:S(2)}, u32[]{:S(2)}) %all-to-all-start) | async-done | bytes 524320 | tf_op jit(solution)/shard_map/all_to_all | solution.py:94
  114.2 9.3 %reshape.427 = f32[8,1,32768]{2,1,0:T(1,128)S(1)} reshape(f32[2048,2,4,16]{3,2,1,0:T(4,128)} %bitcast.433) | data formatting | bytes 2097152
  123.5 31.6 %all_to_all.198 = f32[8,1,32768]{2,1,0:T(1,128)S(1)} all-to-all(f32[8,1,32768]{2,1,0:T(1,128)S(1)} %reshape.427), channel_id=1, replica_groups=mesh['sy'=8,'sx'=32] {'sy'}, dimensions={0} | all-to-all | bytes 2097152 | tf_op jit(solution)/shard_map/all_to_all | solution.py:98
  158.7 9.0 %reshape.428 = f32[2048,2,4,16]{3,2,1,0:T(4,128)} reshape(f32[8,32768]{1,0:T(8,128)S(1)} %reduce.5) | data formatting | bytes 2097152
  182.1 16.8 %all-to-all-done.2 = f32[2,4,256,128]{3,1,0,2:T(4,128)S(1)} async-done(((f32[2,4,256,128]{3,1,0,2:T(4,128)}), f32[2,4,256,128]{3,1,0,2:T(4,128)S(1)}, u32[]{:S(2)}, u32[]{:S(2)}) %all-to-all-start.2) | async-done | bytes 1048608 | tf_op jit(solution)/shard_map/all_to_all | solution.py:99
  216.2 16.5 %reduce.6 = f32[4096,2,8]{2,1,0:T(2,128)} reduce(f32[4096,2,1,8]{3,2,1,0:T(1,128)} %bitcast.437, f32[]{:T(128)} %broadcast.757), dimensions={2}, to_apply=%bitcast.397.reduce_sub_computation | reduce | bytes 524292
  232.7 7.2 %reshape.429 = f32[32,1,2048]{2,1,0:T(1,128)S(1)} reshape(f32[4096,2,8]{2,1,0:T(2,128)} %reduce.6) | data formatting | bytes 524288
  239.9 12.4 %all_to_all.199 = f32[32,1,2048]{2,1,0:T(1,128)S(1)} all-to-all(f32[32,1,2048]{2,1,0:T(1,128)S(1)} %reshape.429), channel_id=1, replica_groups=mesh['sy'=8,'sx'=32] {'sx'}, dimensions={0} | all-to-all | bytes 524288 | tf_op jit(solution)/shard_map/all_to_all | solution.py:107
  253.5 8.3 %reshape.430 = f32[4096,2,1,8]{3,2,1,0:T(1,128)} reshape(f32[32,2048]{1,0:T(8,128)S(1)} %reduce.7) | data formatting | bytes 524288
  261.8 8.0 %copy.152 = f32[2,1,8,4096]{3,1,2,0:T(1,128)S(1)} copy(f32[2,1,8,4096]{2,1,0,3:T(1,128)} %bitcast.438) | data formatting | bytes 524288 | tf_op jit(solution)/shard_map/all_to_all | solution.py:107
  274.5 12.2 %all-to-all-done.4 = f32[2,1,128,256]{3,0,1,2:T(2,128)S(1)} async-done(((f32[2,1,128,256]{3,0,1,2:T(2,128)}), f32[2,1,128,256]{3,0,1,2:T(2,128)S(1)}, u32[]{:S(2)}, u32[]{:S(2)}) %all-to-all-start.4) | async-done | bytes 262176 | tf_op jit(solution)/shard_map/all_to_all | solution.py:108
  290.1 9.3 %reduce.8 = f32[2048,16]{1,0:T(8,128)S(1)} reduce(f32[2048,1,1,16]{3,2,1,0:T(1,128)S(1)} %bitcast.448, f32[]{:T(128)} %broadcast.757), dimensions={1,2}, to_apply=%bitcast.399.reduce_sub_computation | reduce | bytes 262148
  315.2 10.7 %all_to_all.200 = f32[1,1,128,256]{3,1,0,2:T(1,128)S(1)} all-to-all(f32[1,1,128,256]{3,1,0,2:T(1,128)S(1)} %copy.163), channel_id=1, replica_groups=mesh['sy'=8,'sx'=32] {'sy'}, dimensions={2} | all-to-all | bytes 262144 | tf_op jit(solution)/shard_map/all_to_all | solution.py:94
  335.5 12.7 %all_to_all.201 = f32[8,1,8192]{2,1,0:T(1,128)S(1)} all-to-all(f32[8,1,8192]{2,1,0:T(1,128)} %reshape.433), channel_id=1, replica_groups=mesh['sy'=8,'sx'=32] {'sy'}, dimensions={0} | all-to-all | bytes 524288 | tf_op jit(solution)/shard_map/all_to_all | solution.py:98
  356.9 16.4 %all_to_all.202 = f32[2,1,256,128]{3,0,1,2:T(2,128)S(1)} all-to-all(f32[2,1,256,128]{3,0,1,2:T(2,128)S(1)} %copy.168), channel_id=1, replica_groups=mesh['sy'=8,'sx'=32] {'sx'}, dimensions={2} | all-to-all | bytes 524288 | tf_op jit(solution)/shard_map/all_to_all | solution.py:99
  383.7 11.2 %copy.171 = f32[2,4,8,4096]{2,1,0,3:T(4,128)} copy(f32[2,4,8,4096]{3,2,1,0:T(8,128)S(1)} %pad_maximum_fusion.1) | data formatting | bytes 2097152 | tf_op jit(solution)/shard_map/stack | solution.py:90
  394.9 21.3 %reshape.435 = f32[32,1,8192]{2,1,0:T(1,128)S(1)} reshape(f32[4096,2,4,8]{3,2,1,0:T(4,128)} %bitcast.431) | data formatting | bytes 2097152
  416.2 20.9 %all_to_all.203 = f32[32,1,8192]{2,1,0:T(1,128)S(1)} all-to-all(f32[32,1,8192]{2,1,0:T(1,128)S(1)} %reshape.435), channel_id=1, replica_groups=mesh['sy'=8,'sx'=32] {'sx'}, dimensions={0} | all-to-all | bytes 2097152 | tf_op jit(solution)/shard_map/all_to_all | solution.py:107
  440.3 21.8 %reshape.436 = f32[4096,2,4,8]{3,2,1,0:T(4,128)} reshape(f32[32,8192]{1,0:T(8,128)S(1)} %reduce.11) | data formatting | bytes 2097152
  462.1 12.5 %copy.203 = f32[2,4,8,32,128]{4,2,3,1,0:T(8,128)S(1)} copy(f32[2,4,8,32,128]{2,1,0,4,3:T(4,128)} %bitcast.432) | data formatting | bytes 2097152 | tf_op jit(solution)/shard_map/all_to_all | solution.py:107
  475.1 31.9 %all_to_all.204 = f32[2,4,128,256]{3,1,0,2:T(4,128)S(1)} all-to-all(f32[2,4,128,256]{3,1,0,2:T(4,128)S(1)} %copy.174), channel_id=1, replica_groups=mesh['sy'=8,'sx'=32] {'sy'}, dimensions={2} | all-to-all | bytes 2097152 | tf_op jit(solution)/shard_map/all_to_all | solution.py:108
  527.0 8.0 %collective-permute-done = f32[1,128]{1,0:T(1,128)S(1)} collective-permute-done((f32[1,128]{1,0:T(1,128)S(1)}, f32[1,128]{1,0:T(1,128)S(1)}, u32[]{:S(2)}, u32[]{:S(2)}) %collective-permute-start) | collective-permute-done | bytes 544 | tf_op jit(solution)/shard_map/ppermute | solution.py:18
  (167 shorter events, 159.0 us)
Async XLA Ops:
  7.2 59.3 %all-gather.3.cloned.1.call-start = ((), (), s32[]{:S(2)}) async-start(), calls=%async_computation.12 | async-start | bytes 4325376 | tf_op jit(solution)/shard_map/all_gather | solution.py:135
  73.4 3.9 copy-start.2
  76.4 0.8 copy-start
  78.4 24.7 %all-to-all-start = ((f32[1,4,128,256]{3,1,0,2:T(4,128)}), f32[1,4,128,256]{3,1,0,2:T(4,128)S(1)}, u32[]{:S(2)}, u32[]{:S(2)}) async-start(f32[1,4,128,256]{3,1,0,2:T(4,128)} %copy.142), calls=%async_computation | async-start | bytes 1048576 | tf_op jit(solution)/shard_map/all_to_all | solution.py:94
  174.3 7.7 %copy-start.3 = (f32[4,2,8,4096]{3,2,1,0:T(8,128)S(1)}, f32[4,2,8,4096]{3,2,1,0:T(8,128)}, u32[]{:S(2)}) copy-start(f32[4,2,8,4096]{3,2,1,0:T(8,128)} %param.13) | copy-start | bytes 3145732
  175.7 23.3 %all-to-all-start.2 = ((f32[2,4,256,128]{3,1,0,2:T(4,128)}), f32[2,4,256,128]{3,1,0,2:T(4,128)S(1)}, u32[]{:S(2)}, u32[]{:S(2)}) async-start(f32[2,4,256,128]{3,1,0,2:T(4,128)} %copy.148), calls=%async_computation.2 | async-start | bytes 2097152 | tf_op jit(solution)/shard_map/all_to_all | solution.py:99
  270.8 15.9 %all-to-all-start.4 = ((f32[2,1,128,256]{3,0,1,2:T(2,128)}), f32[2,1,128,256]{3,0,1,2:T(2,128)S(1)}, u32[]{:S(2)}, u32[]{:S(2)}) async-start(f32[2,1,128,256]{3,0,1,2:T(2,128)} %copy.154), calls=%async_computation.4 | async-start | bytes 524288 | tf_op jit(solution)/shard_map/all_to_all | solution.py:108
  300.4 11.5 %all-to-all-start.5 = ((f32[8,1,4096]{2,1,0:T(1,128)}), f32[8,1,4096]{2,1,0:T(1,128)S(1)}, u32[]{:S(2)}, u32[]{:S(2)}) async-start(f32[8,1,4096]{2,1,0:T(1,128)} %reshape.431), calls=%async_computation.5 | async-start | bytes 262144 | tf_op jit(solution)/shard_map/all_to_all | solution.py:112
  520.7 24.1 %all-to-all-start.11 = ((f32[8,1,16384]{2,1,0:T(1,128)}), f32[8,1,16384]{2,1,0:T(1,128)S(1)}, u32[]{:S(2)}, u32[]{:S(2)}) async-start(f32[8,1,16384]{2,1,0:T(1,128)} %reshape.437), calls=%async_computation.11 | async-start | bytes 1048576 | tf_op jit(solution)/shard_map/all_to_all | solution.py:112
  524.2 10.7 %collective-permute-start = (f32[1,128]{1,0:T(1,128)S(1)}, f32[1,128]{1,0:T(1,128)S(1)}, u32[]{:S(2)}, u32[]{:S(2)}) collective-permute-start(f32[1,128]{1,0:T(1,128)S(1)} %get-tuple-element.24), channel_id=1, source_target_pairs={{0,32},{32,64},{64,96},{96,128},{128,160},{160,192},{192,224},{224... | collective-permute-start | bytes 1544 | tf_op jit(solution)/shard_map/ppermute | solution.py:18
  525.5 11.5 %collective-permute-start.1 = (f32[1,128]{1,0:T(1,128)S(1)}, f32[1,128]{1,0:T(1,128)S(1)}, u32[]{:S(2)}, u32[]{:S(2)}) collective-permute-start(f32[1,128]{1,0:T(1,128)S(1)} %get-tuple-element.25), channel_id=1, source_target_pairs={{32,0},{64,32},{96,64},{128,96},{160,128},{192,160},{224,192},{0,2... | collective-permute-start | bytes 1544 | tf_op jit(solution)/shard_map/ppermute | solution.py:21
  537.2 3.9 collective-permute-start.3
  539.1 4.7 collective-permute-start.2
  546.5 8.5 %copy-start.1 = (f32[1,8,128,128]{3,2,1,0:T(8,128)S(1)}, f32[1,8,128,128]{3,2,1,0:T(8,128)}, u32[]{:S(2)}) copy-start(f32[1,8,128,128]{3,2,1,0:T(8,128)} %copy-done) | copy-start | bytes 1572868
Sparse Core Ops, SparseCore 0:
  11.1 55.2 all-gather.2
where the time goes:
time: 574 us; the launch traced here: 563 us
  local copies, waits for them, and re-layouts  181 us (32%)
  blocking collectives  137 us (24%)
  waiting for transfers between devices  123 us (21%)
  other arithmetic  42 us (7%)
  matrix products  36.7 us (6%)
  starting transfers between devices  28.4 us (5%)
  between operations  15.5 us (3%)
    unnamed x28, local copies, waits for them, and re-layouts  110 us
    all_gather x1, waiting for transfers between devices, on_device(): piece = lax.all_gather(flat_tiles, 'sx', axis=0, tiled=True)  56 us
    all_to_all x2, blocking collectives, to_spectra(): lax.all_to_all(along_y, 'sy', split_axis=3, concat_axis=2, tiled=True)  44.3 us
    dot_general x56, matrix products, contract(): return jnp.einsum(pattern, operand, matrix, precision=highest)  33.8 us
    all_to_all x2, blocking collectives, from_spectra(): lax.all_to_all(along_x, 'sx', split_axis=3, concat_axis=2, tiled=True)  33.3 us
    all_to_all x1, blocking collectives, from_spectra(): lax.all_to_all(jnp.swapaxes(blocks, 2, 3), 'sy', split_axis=2, concat_axi...  31.9 us
    unnamed x2, other arithmetic  25.8 us
    all_to_all x3, local copies, waits for them, and re-layouts, from_spectra(): lax.all_to_all(along_x, 'sx', split_axis=3, concat_axis=2, tiled=True)  20.7 us
  transfers between devices with their start and end apart: 10, of which 9 were waited for; matrix products, arithmetic and copies ran while one was open for 1% of the time, Pallas kernels for 0%

commit v1 on v0

v1 whole, which is shorter than its diff:
```python
import math

import jax
import jax.numpy as jnp
import numpy as np
from jax import lax
from jax.experimental import pallas as pl
from jax.experimental.pallas import tpu as pltpu
from jax.sharding import PartitionSpec as P

highest = lax.Precision.HIGHEST
tv_weight = 0.5
smoothing = 0.25
f32 = jnp.float32
SHORT, LANES, ROWS, PIECE = 32, 128, 8, 16
DEVICES = 256
NX, NY = 4096, 2048
EVERY = ("sy", "sx")


def table(array):
    return np.asarray(array, np.float32)


def circle(left, right, length):
    angles = np.outer(np.arange(left), np.arange(right)) % length * (2.0 * np.pi / length)
    return np.cos(angles), np.sin(angles)


def joined(cos, sin, sign):
    return table(np.block([[cos, sign * sin], [-sign * sin, cos]]))


def make_tables():
    cos_turn, sin_turn = circle(SHORT, LANES, NX)
    cos_long, sin_long = circle(LANES, LANES, LANES)
    cos_dev, sin_dev = circle(DEVICES, DEVICES, DEVICES)
    cos_row, sin_row = circle(DEVICES, ROWS, NY)
    cos_eight, sin_eight = circle(ROWS, ROWS, ROWS)
    spread = np.eye(PIECE)
    wide = lambda matrix: np.kron(matrix, spread)
    lane = np.arange(LANES)
    kappa = np.arange(DEVICES)
    flip = np.zeros((LANES, LANES))
    flip[LANES - 1 - lane, lane] = 1.0
    flip_first = np.zeros((LANES, LANES))
    flip_first[(LANES - lane) % LANES, lane] = 1.0
    flip_rows = np.zeros((DEVICES, DEVICES))
    flip_rows[kappa, (DEVICES - kappa) % DEVICES] = 1.0
    lam = np.arange(ROWS)
    flip_lam = np.zeros((ROWS, ROWS))
    flip_lam[ROWS - 1 - lam, lam] = 1.0
    flip_lam_first = np.zeros((ROWS, ROWS))
    flip_lam_first[(ROWS - lam) % ROWS, lam] = 1.0
    return dict(
        turn_x=table(np.stack([cos_turn, sin_turn])),
        x_forward=joined(cos_long, sin_long, -1.0),
        x_inverse=joined(cos_long, sin_long, 1.0),
        y_long=table(np.concatenate([cos_dev, sin_dev])),
        turn_y=table(
            np.stack([np.repeat(cos_row, PIECE, axis=1), np.repeat(sin_row, PIECE, axis=1)])
        ),
        y_forward=joined(wide(cos_eight), wide(sin_eight), -1.0),
        y_inverse=joined(wide(cos_eight), wide(sin_eight), 1.0),
        flips=table(np.stack([flip, flip_first])),
        flip_rows=table(flip_rows),
        flip_lams=table(np.stack([wide(flip_lam), wide(flip_lam_first)])),
    )


def dot(left, right):
    return jnp.dot(left, right, precision=highest, preferred_element_type=f32)


def run(body, shapes, *operands, scalars=0, scratch=()):
    whole = pl.BlockSpec(memory_space=pltpu.VMEM)
    single = not isinstance(shapes, (list, tuple))
    return pl.pallas_call(
        body,
        out_shape=shapes,
        in_specs=[pl.BlockSpec(memory_space=pltpu.SMEM)] * scalars
        + [whole] * (len(operands) - scalars),
        out_specs=whole if single else [whole] * len(shapes),
        scratch_shapes=list(scratch),
        compiler_params=pltpu.CompilerParams(vmem_limit_bytes=48 * 1024 * 1024),
    )(*operands)


def shaped(*dims, dtype=f32):
    return jax.ShapeDtypeStruct(dims, dtype)


def swap_blocks(field):
    sub = lax.broadcasted_iota(jnp.int32, field.shape, 1)
    group = lax.broadcasted_iota(jnp.int32, field.shape, 2) // PIECE
    for step in (1, 2, 4):
        low = (sub & step) == 0
        shift = PIECE * step
        if step == 4:
            other = pltpu.roll(pltpu.roll(field, shift, 2), step, 1)
        else:
            moved = jnp.where(
                low, pltpu.roll(field, LANES - shift, 2), pltpu.roll(field, shift, 2)
            )
            other = jnp.where(
                low, pltpu.roll(moved, ROWS - step, 1), pltpu.roll(moved, step, 1)
            )
        field = jnp.where(low == ((group & step) == 0), field, other)
    return field


def add(left, right):
    if left is None or right is None:
        return right if left is None else left
    return left + right


def subtract(left, right):
    if right is None:
        return left
    return -right if left is None else left - right


def scaled(value, factor):
    return None if value is None else value * f32(factor)


def turned(real, imag, cos, sin):
    return (
        subtract(scaled(real, cos), scaled(imag, sin)),
        add(scaled(real, sin), scaled(imag, cos)),
    )


def short_transform(points, sign):
    length = len(points)
    if length == 1:
        return points
    even = short_transform(points[0::2], sign)
    odd = short_transform(points[1::2], sign)
    low, high = [], []
    for k in range(length // 2):
        real, imag = odd[k]
        if k == 0:
            part = (real, imag)
        elif 4 * k == length:
            part = (
                (None if imag is None else imag * f32(-sign)),
                (None if real is None else real * f32(sign)),
            )
        else:
            angle = 2.0 * math.pi * k / length
            part = turned(real, imag, math.cos(angle), sign * math.sin(angle))
        low.append((add(even[k][0], part[0]), add(even[k][1], part[1])))
        high.append((subtract(even[k][0], part[0]), subtract(even[k][1], part[1])))
    return low + high


def rows_to_lines(points, turn, matrix, work):
    for c, (real, imag) in enumerate(short_transform(points, -1.0)):
        cos, sin = turn[0, c : c + 1, :], turn[1, c : c + 1, :]
        imag = jnp.zeros_like(real) if imag is None else imag
        work[ROWS * c : ROWS * (c + 1), :LANES] = real * cos + imag * sin
        work[ROWS * c : ROWS * (c + 1), LANES:] = imag * cos - real * sin
    lines = dot(work[...], matrix[...])
    return [
        swap_blocks(part.reshape(SHORT, ROWS, LANES)).reshape(DEVICES, LANES)
        for part in (lines[:, :LANES], lines[:, LANES:])
    ]


def lines_to_rows(real, imag, turn, matrix, work):
    parts = [
        swap_blocks(part.reshape(SHORT, ROWS, LANES)).reshape(DEVICES, LANES)
        for part in (real, imag)
    ]
    work[...] = dot(jnp.concatenate(parts, axis=1), matrix[...])
    points = []
    for c in range(SHORT):
        cos, sin = turn[0, c : c + 1, :], turn[1, c : c + 1, :]
        real = work[ROWS * c : ROWS * (c + 1), :LANES]
        imag = work[ROWS * c : ROWS * (c + 1), LANES:]
        points.append((real * cos - imag * sin, real * sin + imag * cos))
    return short_transform(points, 1.0)


def forward_y(received, fields, y_long, turn_y, matrix):
    stacked = jnp.concatenate(
        [received[pl.ds(f, DEVICES, stride=fields), :] for f in range(fields)], axis=1
    )
    both = dot(y_long[...], stacked)
    by_cos, by_sin = both[:DEVICES], both[DEVICES:]
    cos, sin = turn_y[0], turn_y[1]
    spectra = []
    for f in range(0, fields, 2):
        at_real = slice(f * LANES, (f + 1) * LANES)
        at_imag = slice((f + 1) * LANES, (f + 2) * LANES)
        real = by_cos[:, at_real] + by_sin[:, at_imag]
        imag = by_cos[:, at_imag] - by_sin[:, at_real]
        lines = jnp.concatenate([real * cos + imag * sin, imag * cos - real * sin], axis=1)
        out = dot(lines, matrix[...])
        spectra.append((out[:, :LANES], out[:, LANES:]))
    return spectra


def inverse_y(spectra, y_long, turn_y, matrix, sent):
    cos, sin = turn_y[0], turn_y[1]
    columns = []
    for real, imag in spectra:
        lines = dot(jnp.concatenate([real, imag], axis=1), matrix[...])
        real, imag = lines[:, :LANES], lines[:, LANES:]
        columns += [real * cos - imag * sin, real * sin + imag * cos]
    fields = len(columns)
    both = dot(y_long[...], jnp.concatenate(columns, axis=1))
    by_cos, by_sin = both[:DEVICES], both[DEVICES:]
    for f in range(0, fields, 2):
        at_real = slice(f * LANES, (f + 1) * LANES)
        at_imag = slice((f + 1) * LANES, (f + 2) * LANES)
        sent[pl.ds(f, DEVICES, stride=fields), :] = by_cos[:, at_real] - by_sin[:, at_imag]
        sent[pl.ds(f + 1, DEVICES, stride=fields), :] = by_cos[:, at_imag] + by_sin[:, at_real]


def pack_tiles(tiles, sent):
    for piece in range(PIECE):
        rows = jnp.concatenate(
            [
                tiles[l, ROWS * piece : ROWS * (piece + 1), :].astype(f32)
                for l in range(tiles.shape[0])
            ],
            axis=0,
        ).astype(jnp.bfloat16)
        sent[piece] = rows
        sent[piece + PIECE] = rows


def pack_pixels(counts, sky, observed, noise, sent):
    lane = lax.broadcasted_iota(jnp.int32, (ROWS, LANES), 1)
    for r in range(SHORT):
        rows = slice(ROWS * r, ROWS * (r + 1))
        sent[r, 0:ROWS, :] = sky[rows, :]
        sent[r, ROWS : 2 * ROWS, :] = observed[rows, :]
        used = lane < counts[r // PIECE]
        weight = noise[rows, :]
        sent[r, 2 * ROWS :, :] = jnp.where(used, -weight, weight)


def first_rows(wanted, tiles, pixels, turn, matrix, sent, coef, pool, work):
    pool[...] = tiles[...].astype(f32)
    for p in range(2):
        points = []
        for b in range(SHORT):
            sky = pixels[b, 0:ROWS, :]
            weight = pixels[b, 2 * ROWS :, :]
            pair = []
            for k in (2 * p, 2 * p + 1):
                start = pl.multiple_of(wanted[4 * b + k] * ROWS, ROWS)
                mask = jnp.where(weight[:, k : k + 1] < 0.0, f32(1.0), f32(0.0))
                value = pool[pl.ds(start, ROWS), :] * mask
                coef[k, b] = value
                pair.append(value * sky)
            points.append(tuple(pair))
        real, imag = rows_to_lines(points, turn, matrix, work)
        sent[pl.ds(2 * p, DEVICES, stride=4), :] = real
        sent[pl.ds(2 * p + 1, DEVICES, stride=4), :] = imag


def middle_lines(received, response, y_long, turn_y, forward, inverse, sent):
    spectra = forward_y(received, 4, y_long, turn_y, forward)
    real = imag = 0.0
    for p, (z_real, z_imag) in enumerate(spectra):
        c_real, c_imag = response[2 * p], response[2 * p + 1]
        real = real + z_real * c_real - z_imag * c_imag
        imag = imag + z_real * c_imag + z_imag * c_real
    inverse_y([(real, imag)], y_long, turn_y, inverse, sent)


def middle_rows(received, pixels, turn, forward, inverse, sent, residual, work):
    points = lines_to_rows(
        received[pl.ds(0, DEVICES, stride=2), :],
        received[pl.ds(1, DEVICES, stride=2), :],
        turn,
        inverse,
        work,
    )
    values = []
    for b in range(SHORT):
        weight = jnp.abs(pixels[b, 2 * ROWS :, :])
        value = weight * (points[b][0] - pixels[b, ROWS : 2 * ROWS, :])
        residual[b] = value
        values.append((value, None))
    real, imag = rows_to_lines(values, turn, forward, work)
    sent[pl.ds(0, DEVICES, stride=2), :] = real
    sent[pl.ds(1, DEVICES, stride=2), :] = imag


def last_lines(received, response, y_long, turn_y, forward, inverse, sent):
    ((real, imag),) = forward_y(received, 2, y_long, turn_y, forward)
    spectra = []
    for p in range(2):
        c_real, c_imag = response[2 * p], response[2 * p + 1]
        spectra.append((real * c_real + imag * c_imag, imag * c_real - real * c_imag))
    inverse_y(spectra, y_long, turn_y, inverse, sent)


def last_rows(received, coef, residual, flow, turn, inverse, sent, work):
    total = None
    for p in range(2):
        points = lines_to_rows(
            received[pl.ds(2 * p, DEVICES, stride=4), :],
            received[pl.ds(2 * p + 1, DEVICES, stride=4), :],
            turn,
            inverse,
            work,
        )
        for b in range(SHORT):
            value = coef[2 * p, b] * points[b][0] + coef[2 * p + 1, b] * points[b][1]
            if p == 0:
                sent[b, 0:ROWS, :] = value + flow[b]
            else:
                sent[b, 0:ROWS, :] += value
    for b in range(SHORT):
        sent[b, ROWS:, :] = residual[b]


def variation(pixels, above, below, flow):
    sky = pixels[:, 0:ROWS, :]
    lane = lax.broadcasted_iota(jnp.int32, sky.shape, 2)
    sub = lax.broadcasted_iota(jnp.int32, sky.shape, 1)

    def after(field):
        moved = pltpu.roll(field, LANES - 1, 2)
        following = jnp.concatenate([moved[1:], moved[:1]], axis=0)
        return jnp.where(lane == LANES - 1, following, moved)

    def flows(field, following):
        step_x = after(field) - field
        step_y = following - field
        magnitude = jnp.sqrt(step_x * step_x + step_y * step_y + smoothing)
        return step_x / magnitude, step_y / magnitude

    upper = jnp.broadcast_to(above[...].reshape(SHORT, 1, LANES), sky.shape)
    lower = jnp.broadcast_to(below[...].reshape(SHORT, 1, LANES), sky.shape)
    following = jnp.where(sub == ROWS - 1, lower, pltpu.roll(sky, ROWS - 1, 1))
    flow_x, flow_y = flows(sky, following)
    _, upper_y = flows(upper, sky)
    moved = pltpu.roll(flow_x, 1, 2)
    before_x = jnp.where(
        lane == 0, jnp.concatenate([moved[-1:], moved[:-1]], axis=0), moved
    )
    before_y = jnp.where(sub == 0, upper_y, pltpu.roll(flow_y, 1, 1))
    flow[...] = -tv_weight * (flow_x - before_x + flow_y - before_y)


def pack_transfer(transfer, flips, sent, mirrored):
    for p in range(2):
        for c in range(SHORT):
            at = slice(LANES * c, LANES * (c + 1))
            real_1, imag_1 = transfer[2 * p, 0, :, at], transfer[2 * p, 1, :, at]
            real_2, imag_2 = transfer[2 * p + 1, 0, :, at], transfer[2 * p + 1, 1, :, at]
            rows = slice(ROWS * c, ROWS * (c + 1))
            mirrored[2 * p, rows, :] = real_1 - imag_2
            mirrored[2 * p + 1, rows, :] = imag_1 + real_2
            mirrored[4 + 2 * p, rows, :] = real_1 + imag_2
            mirrored[5 + 2 * p, rows, :] = imag_1 - real_2
    for f in range(4):
        field = mirrored[4 + f].reshape(SHORT, ROWS, LANES)
        sent[pl.ds(f, DEVICES, stride=8), :] = swap_blocks(field).reshape(DEVICES, LANES)
        first = dot(mirrored[f, 0:ROWS, :], flips[1])
        others = dot(mirrored[f], flips[0])
        blocks = [first] + [others[ROWS * c : ROWS * (c + 1)] for c in range(SHORT - 1, 0, -1)]
        field = jnp.stack(blocks)
        sent[pl.ds(4 + f, DEVICES, stride=8), :] = swap_blocks(field).reshape(DEVICES, LANES)


def make_response(received, flip_rows, flip_lams, response, fields):
    def place(v, carry):
        for low in range(2):
            for f in range(8):
                block = received[pl.ds((PIECE * v + low) * 8 + f, ROWS, stride=16), :]
                block = swap_blocks(block.reshape(1, ROWS, LANES)).reshape(ROWS, LANES)
                fields[f, pl.ds(LANES * low + v, ROWS, stride=PIECE), :] = block
        return carry

    lax.fori_loop(0, PIECE, place, 0)
    scale = f32(0.5 / (NX * NY))
    top = lax.broadcasted_iota(jnp.int32, (DEVICES, LANES), 0) == 0
    for f in range(4):
        swapped = dot(flip_rows[...], fields[4 + f])
        mirror = dot(swapped, flip_lams[0])
        first = dot(swapped[0:ROWS], flip_lams[1])
        mirror = jnp.where(top, jnp.broadcast_to(first[0:1], mirror.shape), mirror)
        if f % 2 == 0:
            response[f] = (fields[f] + mirror) * scale
        else:
            response[f] = (fields[f] - mirror) * scale


def exchange(sent, axis, count):
    pieces = sent.reshape(count, sent.size // count // LANES, LANES)
    return lax.all_to_all(pieces, axis, split_axis=0, concat_axis=0, tiled=True).reshape(
        sent.shape
    )


def on_device(sky_image, observed, noise_weight, basis_tiles, intersection, counts, transfer):
    tables = {name: jnp.asarray(value) for name, value in make_tables().items()}
    band, column = lax.axis_index("sy"), lax.axis_index("sx")
    zero = jnp.zeros((), jnp.int32)
    wanted = lax.dynamic_slice(
        intersection, (2 * band + column // PIECE, zero, zero), (1, SHORT, 4)
    ).reshape(SHORT * 4) - band * LANES

    tiles = exchange(
        run(pack_tiles, shaped(SHORT, SHORT, LANES, dtype=jnp.bfloat16), basis_tiles), "sx", SHORT
    )
    pixels = exchange(
        run(
            pack_pixels,
            shaped(SHORT, 3 * ROWS, LANES),
            counts.reshape(2),
            sky_image,
            observed,
            noise_weight,
            scalars=1,
        ),
        "sx",
        SHORT,
    )
    spread = exchange(
        run(
            pack_transfer,
            shaped(DEVICES * 8, LANES),
            transfer,
            tables["flips"],
            scratch=[pltpu.VMEM((8, DEVICES, LANES), f32)],
        ),
        EVERY,
        DEVICES,
    )
    work = [pltpu.VMEM((DEVICES, 2 * LANES), f32)]
    sent, coef = run(
        first_rows,
        [shaped(DEVICES * 4, LANES), shaped(4, SHORT, ROWS, LANES)],
        wanted,
        tiles.reshape(SHORT * SHORT, LANES),
        pixels,
        tables["turn_x"],
        tables["x_forward"],
        scalars=1,
        scratch=[pltpu.VMEM((SHORT * SHORT, LANES), f32)] + work,
    )
    received = exchange(sent, EVERY, DEVICES)

    ahead = [(i, (i + 1) % DEVICES) for i in range(DEVICES)]
    behind = [(target, source) for source, target in ahead]
    above = lax.ppermute(pixels[:, ROWS - 1, :], EVERY, ahead)
    below = lax.ppermute(pixels[:, 0, :], EVERY, behind)
    flow = run(variation, shaped(SHORT, ROWS, LANES), pixels, above, below)
    response = run(
        make_response,
        shaped(4, DEVICES, LANES),
        spread,
        tables["flip_rows"],
        tables["flip_lams"],
        scratch=[pltpu.VMEM((8, DEVICES, LANES), f32)],
    )
    y_tables = [tables[name] for name in ("y_long", "turn_y", "y_forward", "y_inverse")]
    x_tables = [tables[name] for name in ("turn_x", "x_forward", "x_inverse")]
    sent = run(middle_lines, shaped(DEVICES * 2, LANES), received, response, *y_tables)
    received = exchange(sent, EVERY, DEVICES)
    sent, residual = run(
        middle_rows,
        [shaped(DEVICES * 2, LANES), shaped(SHORT, ROWS, LANES)],
        received,
        pixels,
        *x_tables,
        scratch=work,
    )
    received = exchange(sent, EVERY, DEVICES)
    sent = run(last_lines, shaped(DEVICES * 4, LANES), received, response, *y_tables)
    received = exchange(sent, EVERY, DEVICES)
    sent = run(
        last_rows,
        shaped(SHORT, 2 * ROWS, LANES),
        received,
        coef,
        residual,
        flow,
        tables["turn_x"],
        tables["x_inverse"],
        scratch=work,
    )
    blocks = exchange(sent, "sx", SHORT)
    gradient = blocks[:, :ROWS, :].reshape(SHORT * ROWS, LANES)
    residual = blocks[:, ROWS:, :].reshape(SHORT * ROWS, LANES)
    return (residual, gradient)


def solution(mesh):
    placed = (
        P("sy", "sx"),
        P("sy", "sx"),
        P("sy", "sx"),
        P(("sy", "sx"), None, None),
        P(),
        P("sy", "sx"),
        P(None, None, ("sy", "sx"), None),
    )
    return jax.shard_map(
        on_device,
        mesh=mesh,
        in_specs=placed,
        out_specs=(P("sy", "sx"), P("sy", "sx")),
        check_vma=False,
    )
```

time: 574 us -> 197 us (0.34); the launches traced: 563 us -> 196 us
  local copies, waits for them, and re-layouts: 181 us -> 5.51 us
  blocking collectives: 137 us -> 56.1 us
  waiting for transfers between devices: 123 us -> 68.9 us
  other arithmetic: 42 us -> 0.69 us
  matrix products: 36.7 us -> 0 us
  Pallas kernels: 0 us -> 25.5 us
  between operations: 15.5 us -> 0.9 us
  starting transfers between devices: 28.4 us -> 38.5 us
    unnamed x28 -> x46, local copies, waits for them, and re-layouts: 110 us -> 4.58 us
    all_to_all x7 -> x3, blocking collectives: 137 us -> 56.1 us  [exchange(): lax.all_to_all(pieces, axis, split_axis=0, concat_axis=0, tiled=True)]
    all_gather x1 -> x0, waiting for transfers between devices: 56 us -> none  [on_device(): piece = lax.all_gather(flat_tiles, 'sx', axis=0, tiled=True)]
    dot_general x57 -> x0, matrix products: 36.7 us -> none  [the longest x56 33.8 us: contract(): return jnp.einsum(pattern, operand, matrix, precision=highest)]
    all_to_all x16 -> x0, local copies, waits for them, and re-layouts: 35.1 us -> none  [the longest x3 20.7 us: from_spectra(): lax.all_to_all(along_x, 'sx', split_axis=3, concat_axis=2, tiled=True)]
    another operation x16 -> x0, local copies, waits for them, and re-layouts: 26.7 us -> none  [the longest x6 18.2 us: inverse_last(): jnp.stack([out_real, out_imag]).reshape(2, num_fields, num_lines, length)]
    unnamed x2 -> x0, other arithmetic: 25.8 us -> none
    pallas_call x0 -> x10, Pallas kernels: none -> 25.5 us  [run(): pl.pallas_call(body, out_shape=shapes, in_specs=[pl.BlockSpec(memory_spac...]
  transfers between devices with their start and end apart: 10 -> 7, of which waited for: 9 -> 7; matrix products, arithmetic and copies ran while one was open for 1% -> 0% of each run, Pallas kernels for 0% -> 7%
where the time goes in v1:
time: 197 us; the launch traced here: 196 us
  waiting for transfers between devices  68.9 us (35%)
  blocking collectives  56.1 us (28%)
  starting transfers between devices  38.5 us (20%)
  Pallas kernels  25.5 us (13%)
  local copies, waits for them, and re-layouts  5.51 us (3%)
    all_to_all x5, waiting for transfers between devices, exchange(): lax.all_to_all(pieces, axis, split_axis=0, concat_axis=0, tiled=True)  66.1 us
    all_to_all x3, blocking collectives, exchange(): lax.all_to_all(pieces, axis, split_axis=0, concat_axis=0, tiled=True)  56.1 us
    all_to_all x5, starting transfers between devices, exchange(): lax.all_to_all(pieces, axis, split_axis=0, concat_axis=0, tiled=True)  36.1 us
    pallas_call x10, Pallas kernels, run(): pl.pallas_call(body, out_shape=shapes, in_specs=[pl.BlockSpec(memory_spac...  25.5 us
    unnamed x46, local copies, waits for them, and re-layouts  4.58 us
  transfers between devices with their start and end apart: 7, of which 7 were waited for; matrix products, arithmetic and copies ran while one was open for 0% of the time, Pallas kernels for 7%

profile of v1, /device:TPU:1, one launch (start us, length us, event | category | flops | bytes accessed | tf_op | source)
XLA Modules:
  0.0 196.1 jit_solution(6556580680837281601)
XLA Ops:
  2.3 8.7 %all-to-all-start = ((bf16[32,32,128]{2,1,0:T(8,128)(2,1)}), bf16[32,32,128]{2,1,0:T(8,128)(2,1)S(1)}, u32[]{:S(2)}, u32[]{:S(2)}) async-start(bf16[32,32,128]{2,1,0:T(8,128)(2,1)} %shard_map.176), calls=%async_computation | async-start | bytes 524288 | tf_op jit(solution)/shard_map/all_to_all | solution.py:400
  11.1 1.3 shard_map.177
  12.4 7.5 %all-to-all-done = bf16[32,32,128]{2,1,0:T(8,128)(2,1)S(1)} async-done(((bf16[32,32,128]{2,1,0:T(8,128)(2,1)}), bf16[32,32,128]{2,1,0:T(8,128)(2,1)S(1)}, u32[]{:S(2)}, u32[]{:S(2)}) %all-to-all-start) | async-done | bytes 262176 | tf_op jit(solution)/shard_map/all_to_all | solution.py:400
  19.9 3.8 %all-to-all-start.1 = ((f32[32,24,128]{2,1,0:T(8,128)}), f32[32,24,128]{2,1,0:T(8,128)S(1)}, u32[]{:S(2)}, u32[]{:S(2)}) async-start(f32[32,24,128]{2,1,0:T(8,128)} %shard_map.177), calls=%async_computation.1 | async-start | bytes 786432 | tf_op jit(solution)/shard_map/all_to_all | solution.py:400
  23.7 3.0 %shard_map.179 = f32[2048,128]{1,0:T(8,128)} custom-call(f32[4,2,8,4096]{3,2,1,0:T(8,128)S(1)} %copy-done.8, f32[2,128,128]{2,1,0:T(8,128)S(1)} %copy-done.17), custom_call_target="tpu_custom_call" | custom-call | tf_op jit(solution)/shard_map/pallas_call | solution.py:78
  26.7 7.3 %all-to-all-done.1.pixels = f32[32,24,128]{2,1,0:T(8,128)S(1)} async-done(((f32[32,24,128]{2,1,0:T(8,128)}), f32[32,24,128]{2,1,0:T(8,128)S(1)}, u32[]{:S(2)}, u32[]{:S(2)}) %all-to-all-start.1) | async-done | bytes 393248 | tf_op jit(solution)/shard_map/all_to_all | solution.py:400
  34.0 10.8 %all-to-all-start.3 = ((f32[256,8,128]{2,1,0:T(8,128)}), f32[256,8,128]{2,1,0:T(8,128)S(1)}, u32[]{:S(2)}, u32[]{:S(2)}) async-start(f32[256,8,128]{2,1,0:T(8,128)} %bitcast.4), calls=%async_computation.3 | async-start | bytes 2097152 | tf_op jit(solution)/shard_map/all_to_all | solution.py:400
  45.8 3.0 %shard_map.178 = (f32[1024,128]{1,0:T(8,128)}, f32[4,32,8,128]{3,2,1,0:T(8,128)S(1)}) custom-call(s32[128]{0:T(128)S(1)} %sub.15.wanted, bf16[1024,128]{1,0:T(8,128)(2,1)S(1)} %bitcast.25, f32[32,24,128]{2,1,0:T(8,128)S(1)} %all-to-all-done.1.pixels, f32[2,32,128]{2,1,0:T(8,128)S(1)} %copy-done.11, f32[256,256]{1,0:T(8,128)S(1)} %copy-done.6), custom_call_target="tpu_custom_call" | custom-call | tf_op jit(solution)/shard_map/pallas_call | solution.py:78
  49.6 25.8 %all-to-all-done.3 = f32[256,8,128]{2,1,0:T(8,128)S(1)} async-done(((f32[256,8,128]{2,1,0:T(8,128)}), f32[256,8,128]{2,1,0:T(8,128)S(1)}, u32[]{:S(2)}, u32[]{:S(2)}) %all-to-all-start.3) | async-done | bytes 1048608 | tf_op jit(solution)/shard_map/all_to_all | solution.py:400
  75.4 6.5 %all-to-all-start.2 = ((f32[256,4,128]{2,1,0:T(4,128)}), f32[256,4,128]{2,1,0:T(4,128)S(1)}, u32[]{:S(2)}, u32[]{:S(2)}) async-start(f32[256,4,128]{2,1,0:T(4,128)} %bitcast.2), calls=%async_computation.2 | async-start | bytes 1048576 | tf_op jit(solution)/shard_map/all_to_all | solution.py:400
  81.9 0.9 copy-done.13
  83.7 7.0 %shard_map.180.response = f32[4,256,128]{2,1,0:T(8,128)S(1)} custom-call(f32[2048,128]{1,0:T(8,128)S(1)} %bitcast.22, f32[256,256]{1,0:T(8,128)S(1)} %copy-done.13, f32[2,128,128]{2,1,0:T(8,128)S(1)} %copy-done.21), custom_call_target="tpu_custom_call" | custom-call | tf_op jit(solution)/shard_map/pallas_call | solution.py:78
  90.8 11.0 %all-to-all-done.2 = f32[256,4,128]{2,1,0:T(4,128)S(1)} async-done(((f32[256,4,128]{2,1,0:T(4,128)}), f32[256,4,128]{2,1,0:T(4,128)S(1)}, u32[]{:S(2)}, u32[]{:S(2)}) %all-to-all-start.2) | async-done | bytes 524320 | tf_op jit(solution)/shard_map/all_to_all | solution.py:400
  102.8 3.2 %shard_map.181 = f32[512,128]{1,0:T(8,128)S(1)} custom-call(f32[1024,128]{1,0:T(8,128)S(1)} %bitcast.24, f32[4,256,128]{2,1,0:T(8,128)S(1)} %shard_map.180.response, f32[512,256]{1,0:T(8,128)S(1)} %copy-done, f32[2,256,128]{2,1,0:T(8,128)S(1)} %copy-done.2, f32[256,256]{1,0:T(8,128)S(1)} %copy-done.3, f32[256,256]{1,0:T(8,128)S(1)} %copy-done.4), custom_call_target="tpu_custom_call" | custom-call | tf_op jit(solution)/shard_map/pallas_call | solution.py:78
  106.0 21.2 %all_to_all.40 = f32[256,2,128]{2,1,0:T(2,128)S(1)} all-to-all(f32[256,2,128]{2,1,0:T(2,128)S(1)} %bitcast.28), channel_id=1, replica_groups=mesh['sy'=8,'sx'=32] {'sy','sx'}, dimensions={0} | all-to-all | bytes 524288 | tf_op jit(solution)/shard_map/all_to_all | solution.py:400
  127.2 1.9 shard_map.182
  129.2 21.0 %all_to_all.41 = f32[256,2,128]{2,1,0:T(2,128)S(1)} all-to-all(f32[256,2,128]{2,1,0:T(2,128)S(1)} %bitcast.29), channel_id=1, replica_groups=mesh['sy'=8,'sx'=32] {'sy','sx'}, dimensions={0} | all-to-all | bytes 524288 | tf_op jit(solution)/shard_map/all_to_all | solution.py:400
  150.2 3.6 %shard_map.183 = f32[1024,128]{1,0:T(8,128)} custom-call(f32[512,128]{1,0:T(8,128)S(1)} %bitcast.26, f32[4,256,128]{2,1,0:T(8,128)S(1)} %shard_map.180.response, f32[512,256]{1,0:T(8,128)S(1)} %copy-done, f32[2,256,128]{2,1,0:T(8,128)S(1)} %copy-done.2, f32[256,256]{1,0:T(8,128)S(1)} %copy-done.3, f32[256,256]{1,0:T(8,128)S(1)} %copy-done.5), custom_call_target="tpu_custom_call" | custom-call | tf_op jit(solution)/shard_map/pallas_call | solution.py:78
  153.8 6.2 %all-to-all-start.6 = ((f32[256,4,128]{2,1,0:T(4,128)}), f32[256,4,128]{2,1,0:T(4,128)S(1)}, u32[]{:S(2)}, u32[]{:S(2)}) async-start(f32[256,4,128]{2,1,0:T(4,128)} %bitcast.10), calls=%async_computation.6 | async-start | bytes 1048576 | tf_op jit(solution)/shard_map/all_to_all | solution.py:400
  160.1 1.7 collective-permute-start
  163.2 2.2 %collective-permute-done.1.below = f32[32,128]{1,0:T(8,128)S(1)} collective-permute-done((f32[32,128]{1,0:T(8,128)S(1)}, f32[32,128]{1,0:T(8,128)S(1)}, u32[]{:S(2)}, u32[]{:S(2)}) %collective-permute-start.1) | collective-permute-done | bytes 16416 | tf_op jit(solution)/shard_map/ppermute | solution.py:457
  165.6 14.5 %all-to-all-done.6 = f32[256,4,128]{2,1,0:T(4,128)S(1)} async-done(((f32[256,4,128]{2,1,0:T(4,128)}), f32[256,4,128]{2,1,0:T(4,128)S(1)}, u32[]{:S(2)}, u32[]{:S(2)}) %all-to-all-start.6) | async-done | bytes 524320 | tf_op jit(solution)/shard_map/all_to_all | solution.py:400
  180.1 1.4 shard_map.185
  181.5 13.8 %all_to_all.42 = f32[32,16,128]{2,1,0:T(8,128)S(1)} all-to-all(f32[32,16,128]{2,1,0:T(8,128)S(1)} %shard_map.185), channel_id=1, replica_groups=mesh['sy'=8,'sx'=32] {'sx'}, dimensions={0} | all-to-all | bytes 524288 | tf_op jit(solution)/shard_map/all_to_all | solution.py:400
  (54 shorter events, 7.6 us)
Async XLA Ops:
  1.5 9.5 %copy-start.18 = (f32[256,128]{1,0:T(8,128)S(1)}, f32[256,128]{1,0:T(8,128)}, u32[]{:S(2)}) copy-start(f32[256,128]{1,0:T(8,128)} %sky.1) | copy-start | bytes 393220
  1.5 9.5 %copy-start.19 = (f32[256,128]{1,0:T(8,128)S(1)}, f32[256,128]{1,0:T(8,128)}, u32[]{:S(2)}) copy-start(f32[256,128]{1,0:T(8,128)} %observed.1) | copy-start | bytes 393220
  1.5 9.5 %copy-start.20 = (f32[256,128]{1,0:T(8,128)S(1)}, f32[256,128]{1,0:T(8,128)}, u32[]{:S(2)}) copy-start(f32[256,128]{1,0:T(8,128)} %noise.1) | copy-start | bytes 393220
  1.5 9.5 %copy-start.22 = (s32[2,1]{0,1:T(1,128)S(1)}, s32[2,1]{0,1:T(1,128)}, u32[]{:S(2)}) copy-start(s32[2,1]{0,1:T(1,128)} %param.22) | copy-start | bytes 28
  2.3 21.4 %copy-start.8 = (f32[4,2,8,4096]{3,2,1,0:T(8,128)S(1)}, f32[4,2,8,4096]{3,2,1,0:T(8,128)}, u32[]{:S(2)}) copy-start(f32[4,2,8,4096]{3,2,1,0:T(8,128)} %transfer.1) | copy-start | bytes 3145732
  2.3 17.6 %all-to-all-start = ((bf16[32,32,128]{2,1,0:T(8,128)(2,1)}), bf16[32,32,128]{2,1,0:T(8,128)(2,1)S(1)}, u32[]{:S(2)}, u32[]{:S(2)}) async-start(bf16[32,32,128]{2,1,0:T(8,128)(2,1)} %shard_map.176), calls=%async_computation | async-start | bytes 524288 | tf_op jit(solution)/shard_map/all_to_all | solution.py:400
  12.4 11.3 %copy-start.17 = (f32[2,128,128]{2,1,0:T(8,128)S(1)}, f32[2,128,128]{2,1,0:T(8,128)}, u32[]{:S(2)}) copy-start(f32[2,128,128]{2,1,0:T(8,128)} %constant.58.clone.flips) | copy-start | bytes 393220
  19.9 14.1 %all-to-all-start.1 = ((f32[32,24,128]{2,1,0:T(8,128)}), f32[32,24,128]{2,1,0:T(8,128)S(1)}, u32[]{:S(2)}, u32[]{:S(2)}) async-start(f32[32,24,128]{2,1,0:T(8,128)} %shard_map.177), calls=%async_computation.1 | async-start | bytes 786432 | tf_op jit(solution)/shard_map/all_to_all | solution.py:400
  34.0 11.8 %copy-start.6 = (f32[256,256]{1,0:T(8,128)S(1)}, f32[256,256]{1,0:T(8,128)}, u32[]{:S(2)}) copy-start(f32[256,256]{1,0:T(8,128)} %constant.52.clone.matrix.forward) | copy-start | bytes 786436
  34.0 41.4 %all-to-all-start.3 = ((f32[256,8,128]{2,1,0:T(8,128)}), f32[256,8,128]{2,1,0:T(8,128)S(1)}, u32[]{:S(2)}, u32[]{:S(2)}) async-start(f32[256,8,128]{2,1,0:T(8,128)} %bitcast.4), calls=%async_computation.3 | async-start | bytes 2097152 | tf_op jit(solution)/shard_map/all_to_all | solution.py:400
  75.4 26.4 %all-to-all-start.2 = ((f32[256,4,128]{2,1,0:T(4,128)}), f32[256,4,128]{2,1,0:T(4,128)S(1)}, u32[]{:S(2)}, u32[]{:S(2)}) async-start(f32[256,4,128]{2,1,0:T(4,128)} %bitcast.2), calls=%async_computation.2 | async-start | bytes 1048576 | tf_op jit(solution)/shard_map/all_to_all | solution.py:400
  83.7 18.1 %copy-start = (f32[512,256]{1,0:T(8,128)S(1)}, f32[512,256]{1,0:T(8,128)}, u32[]{:S(2)}) copy-start(f32[512,256]{1,0:T(8,128)} %constant.54.clone.y_long) | copy-start | bytes 1572868
  83.7 18.1 %copy-start.2 = (f32[2,256,128]{2,1,0:T(8,128)S(1)}, f32[2,256,128]{2,1,0:T(8,128)}, u32[]{:S(2)}) copy-start(f32[2,256,128]{2,1,0:T(8,128)} %constant.55.clone.turn_y) | copy-start | bytes 786436
  83.7 18.1 %copy-start.3 = (f32[256,256]{1,0:T(8,128)S(1)}, f32[256,256]{1,0:T(8,128)}, u32[]{:S(2)}) copy-start(f32[256,256]{1,0:T(8,128)} %constant.56.clone.forward) | copy-start | bytes 786436
  102.8 24.4 %copy-start.12 = (f32[2,32,128]{2,1,0:T(8,128)S(1)}, f32[2,32,128]{2,1,0:T(8,128)}, u32[]{:S(2)}) copy-start(f32[2,32,128]{2,1,0:T(8,128)} %constant.51.clone.turn) | copy-start | bytes 98308
  105.9 21.3 %copy-start.1 = (f32[256,256]{1,0:T(8,128)S(1)}, f32[256,256]{1,0:T(8,128)}, u32[]{:S(2)}) copy-start(f32[256,256]{1,0:T(8,128)} %constant.53.clone.inverse) | copy-start | bytes 786436
  106.0 21.2 %copy-start.7 = (f32[256,256]{1,0:T(8,128)S(1)}, f32[256,256]{1,0:T(8,128)}, u32[]{:S(2)}) copy-start(f32[256,256]{1,0:T(8,128)} %constant.52.clone.matrix.forward) | copy-start | bytes 786436
  129.1 21.1 %copy-start.14 = (f32[32,8,128]{2,1,0:T(8,128)}, f32[32,8,128]{2,1,0:T(8,128)S(1)}, u32[]{:S(2)}) copy-start(f32[32,8,128]{2,1,0:T(8,128)S(1)} %get-tuple-element.9.residual) | copy-start | bytes 393220
  129.1 21.1 %copy-start.5 = (f32[256,256]{1,0:T(8,128)S(1)}, f32[256,256]{1,0:T(8,128)}, u32[]{:S(2)}) copy-start(f32[256,256]{1,0:T(8,128)} %constant.57.clone.inverse) | copy-start | bytes 786436
  153.8 26.3 %copy-start.15 = (f32[32,8,128]{2,1,0:T(8,128)S(1)}, f32[32,8,128]{2,1,0:T(8,128)}, u32[]{:S(2)}) copy-start(f32[32,8,128]{2,1,0:T(8,128)} %copy-done.14) | copy-start | bytes 393220
  153.8 26.3 %all-to-all-start.6 = ((f32[256,4,128]{2,1,0:T(4,128)}), f32[256,4,128]{2,1,0:T(4,128)S(1)}, u32[]{:S(2)}, u32[]{:S(2)}) async-start(f32[256,4,128]{2,1,0:T(4,128)} %bitcast.10), calls=%async_computation.6 | async-start | bytes 1048576 | tf_op jit(solution)/shard_map/all_to_all | solution.py:400
  160.1 20.1 %copy-start.10 = (f32[4,32,8,128]{3,2,1,0:T(8,128)S(1)}, f32[4,32,8,128]{3,2,1,0:T(8,128)}, u32[]{:S(2)}) copy-start(f32[4,32,8,128]{3,2,1,0:T(8,128)} %copy-done.9) | copy-start | bytes 1572868
  160.1 3.0 %collective-permute-start = (f32[32,128]{1,0:T(8,128)S(1)}, f32[32,128]{1,0:T(8,128)S(1)}, u32[]{:S(2)}, u32[]{:S(2)}) collective-permute-start(f32[32,128]{1,0:T(8,128)S(1)} %bitcast.32), channel_id=1, source_target_pairs={{0,1},{1,2},{2,3},{3,4},{4,5},{5,6},{6,7},{7,8},{8,9},{9,10},{10,1... | collective-permute-start | bytes 49160 | tf_op jit(solution)/shard_map/ppermute | solution.py:456
  161.8 3.5 %collective-permute-start.1 = (f32[32,128]{1,0:T(8,128)S(1)}, f32[32,128]{1,0:T(8,128)S(1)}, u32[]{:S(2)}, u32[]{:S(2)}) collective-permute-start(f32[32,128]{1,0:T(8,128)S(1)} %bitcast.31), channel_id=1, source_target_pairs={{1,0},{2,1},{3,2},{4,3},{5,4},{6,5},{7,6},{8,7},{9,8},{10,9},{11,1... | collective-permute-start | bytes 49160 | tf_op jit(solution)/shard_map/ppermute | solution.py:457
  (6 other events, 5.4 us)

commit v2 on v1

--- a/solution.py
+++ b/solution.py
@@ -14,6 +14,8 @@
 f32 = jnp.float32
 SHORT, LANES, ROWS, PIECE = 32, 128, 8, 16
 DEVICES = 256
+TILE_ROWS = 32
+CODE_BITS = 13
 NX, NY = 4096, 2048
 EVERY = ("sy", "sx")
 
@@ -156,6 +158,38 @@
     return low + high
 
 
+def swapped(field):
+    return swap_blocks(field.reshape(SHORT, ROWS, LANES)).reshape(DEVICES, LANES)
+
+
+def encode(values):
+    top = jnp.maximum(
+        jnp.maximum(jnp.abs(values[0]), jnp.abs(values[1])),
+        jnp.maximum(jnp.abs(values[2]), jnp.abs(values[3])),
+    )
+    power = jnp.ceil(jnp.log2(jnp.maximum(top, f32(2.0**-100))))
+    factor = jnp.exp2(f32(CODE_BITS) - power)
+    limit = 2.0**CODE_BITS - 1.0
+    codes = [
+        jnp.clip(jnp.floor(value * factor + 0.5), -limit, limit).astype(jnp.int32)
+        for value in values
+    ]
+    shared = power.astype(jnp.int32) + 128
+    return (
+        (codes[0] << 18) | ((codes[1] & 0x3FFF) << 4) | (shared >> 4),
+        (codes[2] << 18) | ((codes[3] & 0x3FFF) << 4) | (shared & 15),
+    )
+
+
+def decode(first, second):
+    power = (((first & 15) << 4) | (second & 15)) - (128 + CODE_BITS)
+    factor = jnp.exp2(power.astype(f32))
+    return [
+        code.astype(f32) * factor
+        for code in (first >> 18, (first << 14) >> 18, second >> 18, (second << 14) >> 18)
+    ]
+
+
 def rows_to_lines(points, turn, matrix, work):
     for c, (real, imag) in enumerate(short_transform(points, -1.0)):
         cos, sin = turn[0, c : c + 1, :], turn[1, c : c + 1, :]
@@ -163,18 +197,11 @@
         work[ROWS * c : ROWS * (c + 1), :LANES] = real * cos + imag * sin
         work[ROWS * c : ROWS * (c + 1), LANES:] = imag * cos - real * sin
     lines = dot(work[...], matrix[...])
-    return [
-        swap_blocks(part.reshape(SHORT, ROWS, LANES)).reshape(DEVICES, LANES)
-        for part in (lines[:, :LANES], lines[:, LANES:])
-    ]
+    return [lines[:, :LANES], lines[:, LANES:]]
 
 
 def lines_to_rows(real, imag, turn, matrix, work):
-    parts = [
-        swap_blocks(part.reshape(SHORT, ROWS, LANES)).reshape(DEVICES, LANES)
-        for part in (real, imag)
-    ]
-    work[...] = dot(jnp.concatenate(parts, axis=1), matrix[...])
+    work[...] = dot(jnp.concatenate([real, imag], axis=1), matrix[...])
     points = []
     for c in range(SHORT):
         cos, sin = turn[0, c : c + 1, :], turn[1, c : c + 1, :]
@@ -184,15 +211,12 @@
     return short_transform(points, 1.0)
 
 
-def forward_y(received, fields, y_long, turn_y, matrix):
-    stacked = jnp.concatenate(
-        [received[pl.ds(f, DEVICES, stride=fields), :] for f in range(fields)], axis=1
-    )
-    both = dot(y_long[...], stacked)
+def forward_y(received, y_long, turn_y, matrix):
+    both = dot(y_long[...], jnp.concatenate(received, axis=1))
     by_cos, by_sin = both[:DEVICES], both[DEVICES:]
     cos, sin = turn_y[0], turn_y[1]
     spectra = []
-    for f in range(0, fields, 2):
+    for f in range(0, len(received), 2):
         at_real = slice(f * LANES, (f + 1) * LANES)
         at_imag = slice((f + 1) * LANES, (f + 2) * LANES)
         real = by_cos[:, at_real] + by_sin[:, at_imag]
@@ -203,24 +227,45 @@
     return spectra
 
 
-def inverse_y(spectra, y_long, turn_y, matrix, sent):
+def inverse_y(spectra, y_long, turn_y, matrix):
     cos, sin = turn_y[0], turn_y[1]
     columns = []
     for real, imag in spectra:
         lines = dot(jnp.concatenate([real, imag], axis=1), matrix[...])
         real, imag = lines[:, :LANES], lines[:, LANES:]
         columns += [real * cos - imag * sin, real * sin + imag * cos]
-    fields = len(columns)
     both = dot(y_long[...], jnp.concatenate(columns, axis=1))
     by_cos, by_sin = both[:DEVICES], both[DEVICES:]
-    for f in range(0, fields, 2):
+    fields = []
+    for f in range(0, len(columns), 2):
         at_real = slice(f * LANES, (f + 1) * LANES)
         at_imag = slice((f + 1) * LANES, (f + 2) * LANES)
-        sent[pl.ds(f, DEVICES, stride=fields), :] = by_cos[:, at_real] - by_sin[:, at_imag]
-        sent[pl.ds(f + 1, DEVICES, stride=fields), :] = by_cos[:, at_imag] + by_sin[:, at_real]
-
-
-def pack_tiles(tiles, sent):
+        fields.append(by_cos[:, at_real] - by_sin[:, at_imag])
+        fields.append(by_cos[:, at_imag] + by_sin[:, at_real])
+    return fields
+
+
+def every(ref, index, count):
+    return ref[pl.ds(index, DEVICES, stride=count), :]
+
+
+def put(ref, fields, first, count):
+    for f, field in enumerate(fields):
+        ref[pl.ds(first + f, DEVICES, stride=count), :] = field
+
+
+def halves(value):
+    high = value.astype(jnp.bfloat16).astype(f32)
+    return jnp.concatenate([high, value - high], axis=0).astype(jnp.bfloat16)
+
+
+def pixel(parts, b, field):
+    start = TILE_ROWS + 2 * ROWS * field
+    both = parts[b, start : start + 2 * ROWS, :].astype(f32)
+    return both[:ROWS] + both[ROWS:]
+
+
+def pack_inputs(counts, tiles, sky, observed, noise, sent):
     for piece in range(PIECE):
         rows = jnp.concatenate(
             [
@@ -229,28 +274,32 @@
             ],
             axis=0,
         ).astype(jnp.bfloat16)
-        sent[piece] = rows
-        sent[piece + PIECE] = rows
-
-
-def pack_pixels(counts, sky, observed, noise, sent):
+        sent[piece, :TILE_ROWS, :] = rows
+        sent[piece + PIECE, :TILE_ROWS, :] = rows
     lane = lax.broadcasted_iota(jnp.int32, (ROWS, LANES), 1)
     for r in range(SHORT):
         rows = slice(ROWS * r, ROWS * (r + 1))
-        sent[r, 0:ROWS, :] = sky[rows, :]
-        sent[r, ROWS : 2 * ROWS, :] = observed[rows, :]
-        used = lane < counts[r // PIECE]
         weight = noise[rows, :]
-        sent[r, 2 * ROWS :, :] = jnp.where(used, -weight, weight)
-
-
-def first_rows(wanted, tiles, pixels, turn, matrix, sent, coef, pool, work):
-    pool[...] = tiles[...].astype(f32)
+        weight = jnp.where(lane < counts[r // PIECE], -weight, weight)
+        for f, value in enumerate((sky[rows, :], observed[rows, :], weight)):
+            start = TILE_ROWS + 2 * ROWS * f
+            sent[r, start : start + 2 * ROWS, :] = halves(value)
+
+
+def first_rows(wanted, parts, spread, turn, matrix, sent, coef, pixels, top, bottom, pool, work):
+    for h in range(SHORT):
+        pool[TILE_ROWS * h : TILE_ROWS * (h + 1), :] = parts[h, :TILE_ROWS, :].astype(f32)
+    fields = []
     for p in range(2):
         points = []
         for b in range(SHORT):
-            sky = pixels[b, 0:ROWS, :]
-            weight = pixels[b, 2 * ROWS :, :]
+            if p == 0:
+                sky = pixel(parts, b, 0)
+                pixels[b] = sky
+                top[b : b + 1, :] = sky[:1]
+                bottom[b : b + 1, :] = sky[ROWS - 1 :]
+            sky = pixels[b]
+            weight = parts[b, TILE_ROWS + 4 * ROWS : TILE_ROWS + 6 * ROWS, :].astype(f32)[:ROWS]
             pair = []
             for k in (2 * p, 2 * p + 1):
                 start = pl.multiple_of(wanted[4 * b + k] * ROWS, ROWS)
@@ -259,59 +308,54 @@
                 coef[k, b] = value
                 pair.append(value * sky)
             points.append(tuple(pair))
-        real, imag = rows_to_lines(points, turn, matrix, work)
-        sent[pl.ds(2 * p, DEVICES, stride=4), :] = real
-        sent[pl.ds(2 * p + 1, DEVICES, stride=4), :] = imag
-
-
-def middle_lines(received, response, y_long, turn_y, forward, inverse, sent):
-    spectra = forward_y(received, 4, y_long, turn_y, forward)
+        fields += rows_to_lines(points, turn, matrix, work)
+    put(sent, [swapped(word) for word in encode(fields)], 0, 6)
+    put(sent, [spread[word] for word in range(4)], 2, 6)
+
+
+def middle_lines(
+    received, flip_rows, flip_lams, y_long, turn_y, forward, inverse, sent, response, fields
+):
+    make_response(received, flip_rows, flip_lams, response, fields)
+    spectra = forward_y(
+        decode(every(received, 0, 6), every(received, 1, 6)), y_long, turn_y, forward
+    )
     real = imag = 0.0
     for p, (z_real, z_imag) in enumerate(spectra):
         c_real, c_imag = response[2 * p], response[2 * p + 1]
         real = real + z_real * c_real - z_imag * c_imag
         imag = imag + z_real * c_imag + z_imag * c_real
-    inverse_y([(real, imag)], y_long, turn_y, inverse, sent)
-
-
-def middle_rows(received, pixels, turn, forward, inverse, sent, residual, work):
+    put(sent, inverse_y([(real, imag)], y_long, turn_y, inverse), 0, 2)
+
+
+def middle_rows(received, parts, turn, forward, inverse, sent, residual, work):
     points = lines_to_rows(
-        received[pl.ds(0, DEVICES, stride=2), :],
-        received[pl.ds(1, DEVICES, stride=2), :],
-        turn,
-        inverse,
-        work,
+        swapped(every(received, 0, 2)), swapped(every(received, 1, 2)), turn, inverse, work
     )
     values = []
     for b in range(SHORT):
-        weight = jnp.abs(pixels[b, 2 * ROWS :, :])
-        value = weight * (points[b][0] - pixels[b, ROWS : 2 * ROWS, :])
+        value = jnp.abs(pixel(parts, b, 2)) * (points[b][0] - pixel(parts, b, 1))
         residual[b] = value
         values.append((value, None))
-    real, imag = rows_to_lines(values, turn, forward, work)
-    sent[pl.ds(0, DEVICES, stride=2), :] = real
-    sent[pl.ds(1, DEVICES, stride=2), :] = imag
+    fields = rows_to_lines(values, turn, forward, work)
+    put(sent, [swapped(field) for field in fields], 0, 2)
 
 
 def last_lines(received, response, y_long, turn_y, forward, inverse, sent):
-    ((real, imag),) = forward_y(received, 2, y_long, turn_y, forward)
+    ((real, imag),) = forward_y(
+        [every(received, 0, 2), every(received, 1, 2)], y_long, turn_y, forward
+    )
     spectra = []
     for p in range(2):
         c_real, c_imag = response[2 * p], response[2 * p + 1]
         spectra.append((real * c_real + imag * c_imag, imag * c_real - real * c_imag))
-    inverse_y(spectra, y_long, turn_y, inverse, sent)
+    put(sent, encode(inverse_y(spectra, y_long, turn_y, inverse)), 0, 2)
 
 
 def last_rows(received, coef, residual, flow, turn, inverse, sent, work):
-    total = None
+    fields = decode(swapped(every(received, 0, 2)), swapped(every(received, 1, 2)))
     for p in range(2):
-        points = lines_to_rows(
-            received[pl.ds(2 * p, DEVICES, stride=4), :],
-            received[pl.ds(2 * p + 1, DEVICES, stride=4), :],
-            turn,
-            inverse,
-            work,
-        )
+        points = lines_to_rows(fields[2 * p], fields[2 * p + 1], turn, inverse, work)
         for b in range(SHORT):
             value = coef[2 * p, b] * points[b][0] + coef[2 * p + 1, b] * points[b][1]
             if p == 0:
@@ -323,7 +367,7 @@
 
 
 def variation(pixels, above, below, flow):
-    sky = pixels[:, 0:ROWS, :]
+    sky = pixels[...]
     lane = lax.broadcasted_iota(jnp.int32, sky.shape, 2)
     sub = lax.broadcasted_iota(jnp.int32, sky.shape, 1)
 
@@ -362,44 +406,46 @@
             mirrored[2 * p + 1, rows, :] = imag_1 + real_2
             mirrored[4 + 2 * p, rows, :] = real_1 + imag_2
             mirrored[5 + 2 * p, rows, :] = imag_1 - real_2
+    direct, reverse = [], []
     for f in range(4):
-        field = mirrored[4 + f].reshape(SHORT, ROWS, LANES)
-        sent[pl.ds(f, DEVICES, stride=8), :] = swap_blocks(field).reshape(DEVICES, LANES)
+        direct.append(mirrored[4 + f])
         first = dot(mirrored[f, 0:ROWS, :], flips[1])
         others = dot(mirrored[f], flips[0])
         blocks = [first] + [others[ROWS * c : ROWS * (c + 1)] for c in range(SHORT - 1, 0, -1)]
-        field = jnp.stack(blocks)
-        sent[pl.ds(4 + f, DEVICES, stride=8), :] = swap_blocks(field).reshape(DEVICES, LANES)
+        reverse.append(jnp.concatenate(blocks, axis=0))
+    for w, word in enumerate(encode(direct) + encode(reverse)):
+        sent[w] = swapped(word)
 
 
 def make_response(received, flip_rows, flip_lams, response, fields):
-    def place(v, carry):
+    for w in range(4):
+        blocks = [
+            received[pl.ds((PIECE * v + low) * 6 + 2 + w, ROWS, stride=12), :]
+            for low in range(2)
+            for v in range(PIECE)
+        ]
+        word = swap_blocks(jnp.stack(blocks))
         for low in range(2):
-            for f in range(8):
-                block = received[pl.ds((PIECE * v + low) * 8 + f, ROWS, stride=16), :]
-                block = swap_blocks(block.reshape(1, ROWS, LANES)).reshape(ROWS, LANES)
-                fields[f, pl.ds(LANES * low + v, ROWS, stride=PIECE), :] = block
-        return carry
-
-    lax.fori_loop(0, PIECE, place, 0)
+            for v in range(PIECE):
+                fields[w, pl.ds(LANES * low + v, ROWS, stride=PIECE), :] = word[PIECE * low + v]
+    direct = decode(fields[0], fields[1])
+    mirror = dot(flip_rows[...], jnp.concatenate(decode(fields[2], fields[3]), axis=1))
     scale = f32(0.5 / (NX * NY))
     top = lax.broadcasted_iota(jnp.int32, (DEVICES, LANES), 0) == 0
     for f in range(4):
-        swapped = dot(flip_rows[...], fields[4 + f])
-        mirror = dot(swapped, flip_lams[0])
-        first = dot(swapped[0:ROWS], flip_lams[1])
-        mirror = jnp.where(top, jnp.broadcast_to(first[0:1], mirror.shape), mirror)
-        if f % 2 == 0:
-            response[f] = (fields[f] + mirror) * scale
-        else:
-            response[f] = (fields[f] - mirror) * scale
+        lines = mirror[:, f * LANES : (f + 1) * LANES]
+        first = dot(lines[0:ROWS], flip_lams[1])
+        lines = dot(lines, flip_lams[0])
+        lines = jnp.where(top, jnp.broadcast_to(first[0:1], lines.shape), lines)
+        response[f] = (direct[f] + lines if f % 2 == 0 else direct[f] - lines) * scale
 
 
 def exchange(sent, axis, count):
-    pieces = sent.reshape(count, sent.size // count // LANES, LANES)
-    return lax.all_to_all(pieces, axis, split_axis=0, concat_axis=0, tiled=True).reshape(
-        sent.shape
-    )
+    width = sent.size // count
+    shape = (count, 1, width) if width == 6 * LANES else (count, width // LANES, LANES)
+    return lax.all_to_all(
+        sent.reshape(shape), axis, split_axis=0, concat_axis=0, tiled=True
+    ).reshape(sent.shape)
 
 
 def on_device(sky_image, observed, noise_weight, basis_tiles, intersection, counts, transfer):
@@ -410,14 +456,12 @@
         intersection, (2 * band + column // PIECE, zero, zero), (1, SHORT, 4)
     ).reshape(SHORT * 4) - band * LANES
 
-    tiles = exchange(
-        run(pack_tiles, shaped(SHORT, SHORT, LANES, dtype=jnp.bfloat16), basis_tiles), "sx", SHORT
-    )
-    pixels = exchange(
+    parts = exchange(
         run(
-            pack_pixels,
-            shaped(SHORT, 3 * ROWS, LANES),
+            pack_inputs,
+            shaped(SHORT, TILE_ROWS + 6 * ROWS, LANES, dtype=jnp.bfloat16),
             counts.reshape(2),
+            basis_tiles,
             sky_image,
             observed,
             noise_weight,
@@ -426,58 +470,62 @@
         "sx",
         SHORT,
     )
-    spread = exchange(
-        run(
-            pack_transfer,
-            shaped(DEVICES * 8, LANES),
-            transfer,
-            tables["flips"],
-            scratch=[pltpu.VMEM((8, DEVICES, LANES), f32)],
-        ),
-        EVERY,
-        DEVICES,
+    spread = run(
+        pack_transfer,
+        shaped(4, DEVICES, LANES, dtype=jnp.int32),
+        transfer,
+        tables["flips"],
+        scratch=[pltpu.VMEM((8, DEVICES, LANES), f32)],
     )
     work = [pltpu.VMEM((DEVICES, 2 * LANES), f32)]
-    sent, coef = run(
+    sent, coef, pixels, top, bottom = run(
         first_rows,
-        [shaped(DEVICES * 4, LANES), shaped(4, SHORT, ROWS, LANES)],
+        [
+            shaped(DEVICES * 6, LANES, dtype=jnp.int32),
+            shaped(4, SHORT, ROWS, LANES),
+            shaped(SHORT, ROWS, LANES),
+            shaped(SHORT, LANES),
+            shaped(SHORT, LANES),
+        ],
         wanted,
-        tiles.reshape(SHORT * SHORT, LANES),
-        pixels,
+        parts,
+        spread,
         tables["turn_x"],
         tables["x_forward"],
         scalars=1,
-        scratch=[pltpu.VMEM((SHORT * SHORT, LANES), f32)] + work,
+        scratch=[pltpu.VMEM((SHORT * TILE_ROWS, LANES), f32)] + work,
     )
     received = exchange(sent, EVERY, DEVICES)
 
     ahead = [(i, (i + 1) % DEVICES) for i in range(DEVICES)]
     behind = [(target, source) for source, target in ahead]
-    above = lax.ppermute(pixels[:, ROWS - 1, :], EVERY, ahead)
-    below = lax.ppermute(pixels[:, 0, :], EVERY, behind)
+    above = lax.ppermute(bottom, EVERY, ahead)
+    below = lax.ppermute(top, EVERY, behind)
     flow = run(variation, shaped(SHORT, ROWS, LANES), pixels, above, below)
-    response = run(
-        make_response,
-        shaped(4, DEVICES, LANES),
-        spread,
+    y_tables = [tables[name] for name in ("y_long", "turn_y", "y_forward", "y_inverse")]
+    x_tables = [tables[name] for name in ("turn_x", "x_forward", "x_inverse")]
+    sent, response = run(
+        middle_lines,
+        [shaped(DEVICES * 2, LANES), shaped(4, DEVICES, LANES)],
+        received,
         tables["flip_rows"],
         tables["flip_lams"],
-        scratch=[pltpu.VMEM((8, DEVICES, LANES), f32)],
-    )
-    y_tables = [tables[name] for name in ("y_long", "turn_y", "y_forward", "y_inverse")]
-    x_tables = [tables[name] for name in ("turn_x", "x_forward", "x_inverse")]
-    sent = run(middle_lines, shaped(DEVICES * 2, LANES), received, response, *y_tables)
+        *y_tables,
+        scratch=[pltpu.VMEM((4, DEVICES, LANES), jnp.int32)],
+    )
     received = exchange(sent, EVERY, DEVICES)
     sent, residual = run(
         middle_rows,
         [shaped(DEVICES * 2, LANES), shaped(SHORT, ROWS, LANES)],
         received,
-        pixels,
+        parts,
         *x_tables,
         scratch=work,
     )
     received = exchange(sent, EVERY, DEVICES)
-    sent = run(last_lines, shaped(DEVICES * 4, LANES), received, response, *y_tables)
+    sent = run(
+        last_lines, shaped(DEVICES * 2, LANES, dtype=jnp.int32), received, response, *y_tables
+    )
     received = exchange(sent, EVERY, DEVICES)
     sent = run(
         last_rows,

time: 197 us -> 155 us (0.79)
  waiting for transfers between devices: 68.9 us -> 23.2 us
  blocking collectives: 56.1 us -> 91 us
  starting transfers between devices: 38.5 us -> 17.1 us
  Pallas kernels: 25.5 us -> 16.9 us
    all_to_all x5 -> x2, waiting for transfers between devices: 66.1 us -> 20.4 us  [exchange(): lax.all_to_all(sent.reshape(shape), axis, split_axis=0, concat_axis=0, ti...]
    all_to_all x3 -> x4, blocking collectives: 56.1 us -> 91 us  [exchange(): lax.all_to_all(sent.reshape(shape), axis, split_axis=0, concat_axis=0, ti...]
    all_to_all x5 -> x2, starting transfers between devices: 36.1 us -> 14.6 us  [exchange(): lax.all_to_all(sent.reshape(shape), axis, split_axis=0, concat_axis=0, ti...]
    pallas_call x10 -> x8, Pallas kernels: 25.5 us -> 16.9 us  [run(): pl.pallas_call(body, out_shape=shapes, in_specs=[pl.BlockSpec(memory_spac...]
    unnamed x46 -> x32, local copies, waits for them, and re-layouts: 4.58 us -> 4.33 us
  transfers between devices with their start and end apart: 7 -> 4, of which waited for: 7 -> 4; matrix products, arithmetic and copies ran while one was open for 0% -> 1% of each run, Pallas kernels for 7% -> 1%
where the time goes in v2:
time: 155 us
  blocking collectives  91 us (59%)
  waiting for transfers between devices  23.2 us (15%)
  starting transfers between devices  17.1 us (11%)
  Pallas kernels  16.9 us (11%)
  local copies, waits for them, and re-layouts  5.24 us (3%)
    all_to_all x4, blocking collectives, exchange(): lax.all_to_all(sent.reshape(shape), axis, split_axis=0, concat_axis=0, ti...  91 us
    all_to_all x2, waiting for transfers between devices, exchange(): lax.all_to_all(sent.reshape(shape), axis, split_axis=0, concat_axis=0, ti...  20.4 us
    pallas_call x8, Pallas kernels, run(): pl.pallas_call(body, out_shape=shapes, in_specs=[pl.BlockSpec(memory_spac...  16.9 us
    all_to_all x2, starting transfers between devices, exchange(): lax.all_to_all(sent.reshape(shape), axis, split_axis=0, concat_axis=0, ti...  14.6 us
    unnamed x32, local copies, waits for them, and re-layouts  4.33 us
  transfers between devices with their start and end apart: 4, of which 4 were waited for; matrix products, arithmetic and copies ran while one was open for 1% of the time, Pallas kernels for 1%

profile of v2, /device:TPU:1, one launch (start us, length us, event | category | flops | bytes accessed | tf_op | source)
XLA Modules:
  0.0 154.9 jit_solution(2021274019808875100)
XLA Ops:
  1.3 0.9 copy-done.9
  2.2 0.9 copy-done.10
  3.1 0.9 copy-done.11
  4.0 0.9 copy-done.12
  4.9 1.5 shard_map.176
  6.4 8.7 %all-to-all-start = ((bf16[32,80,128]{2,1,0:T(8,128)(2,1)}), bf16[32,80,128]{2,1,0:T(8,128)(2,1)S(1)}, u32[]{:S(2)}, u32[]{:S(2)}) async-start(bf16[32,80,128]{2,1,0:T(8,128)(2,1)} %shard_map.176), calls=%async_computation | async-start | bytes 1310720 | tf_op jit(solution)/shard_map/all_to_all | solution.py:446
  15.2 0.7 dynamic-slice_subtract_fusion
  16.1 1.4 shard_map.177.spread
  17.5 10.5 %all-to-all-done.parts = bf16[32,80,128]{2,1,0:T(8,128)(2,1)S(1)} async-done(((bf16[32,80,128]{2,1,0:T(8,128)(2,1)}), bf16[32,80,128]{2,1,0:T(8,128)(2,1)S(1)}, u32[]{:S(2)}, u32[]{:S(2)}) %all-to-all-start) | async-done | bytes 655392 | tf_op jit(solution)/shard_map/all_to_all | solution.py:446
  28.0 2.0 %shard_map.178 = (s32[1536,128]{1,0:T(8,128)S(1)}, f32[4,32,8,128]{3,2,1,0:T(8,128)S(1)}, f32[32,8,128]{2,1,0:T(8,128)S(1)}, f32[32,128]{1,0:T(8,128)S(1)}, f32[32,128]{1,0:T(8,128)S(1)}) custom-call(s32[128]{0:T(128)S(1)} %sub.15.wanted, bf16[32,80,128]{2,1,0:T(8,128)(2,1)S(1)} %all-to-all-done.parts, s32[4,256,128]{2,1,0:T(8,128)S(1)} %shard_map.177.spread, ...), custom_call_target="tpu_custom_call" | custom-call | tf_op jit(solution)/shard_map/pallas_call | solution.py:80
  30.1 35.7 %all_to_all.30 = s32[256,1,768]{2,1,0:T(1,128)S(1)} all-to-all(s32[256,1,768]{2,1,0:T(1,128)S(1)} %bitcast.17), channel_id=1, replica_groups=mesh['sy'=8,'sx'=32] {'sy','sx'}, dimensions={0} | all-to-all | bytes 1572864 | tf_op jit(solution)/shard_map/all_to_all | solution.py:446
  65.8 4.8 %shard_map.179 = (f32[512,128]{1,0:T(8,128)S(1)}, f32[4,256,128]{2,1,0:T(8,128)S(1)}) custom-call(s32[1536,128]{1,0:T(8,128)S(1)} %bitcast.13, f32[256,256]{1,0:T(8,128)S(1)} %copy-done.8, f32[2,128,128]{2,1,0:T(8,128)S(1)} %copy-done.13, f32[512,256]{1,0:T(8,128)S(1)} %copy-done, f32[2,256,128]{2,1,0:T(8,128)S(1)} %copy-done.1, f32[256,256]{1,0:T(8,128)S(1)} %copy-done.2, ...), custom_call_target="tpu_custom_call" | custom-call | tf_op jit(solution)/shard_map/pallas_call | solution.py:80
  70.7 21.5 %all_to_all.31 = f32[256,2,128]{2,1,0:T(2,128)S(1)} all-to-all(f32[256,2,128]{2,1,0:T(2,128)S(1)} %bitcast.18), channel_id=1, replica_groups=mesh['sy'=8,'sx'=32] {'sy','sx'}, dimensions={0} | all-to-all | bytes 524288 | tf_op jit(solution)/shard_map/all_to_all | solution.py:446
  92.2 1.9 %shard_map.180 = (f32[512,128]{1,0:T(8,128)S(1)}, f32[32,8,128]{2,1,0:T(8,128)S(1)}) custom-call(f32[512,128]{1,0:T(8,128)S(1)} %bitcast.16, bf16[32,80,128]{2,1,0:T(8,128)(2,1)S(1)} %all-to-all-done.parts, f32[2,32,128]{2,1,0:T(8,128)S(1)} %copy-done.7, f32[256,256]{1,0:T(8,128)S(1)} %copy-done.6, f32[256,256]{1,0:T(8,128)S(1)} %copy-done.4), custom_call_target="tpu_custom_call" | custom-call | tf_op jit(solution)/shard_map/pallas_call | solution.py:80
  94.2 20.9 %all_to_all.32 = f32[256,2,128]{2,1,0:T(2,128)S(1)} all-to-all(f32[256,2,128]{2,1,0:T(2,128)S(1)} %bitcast.19), channel_id=1, replica_groups=mesh['sy'=8,'sx'=32] {'sy','sx'}, dimensions={0} | all-to-all | bytes 524288 | tf_op jit(solution)/shard_map/all_to_all | solution.py:446
  115.1 3.7 %shard_map.181 = s32[512,128]{1,0:T(8,128)} custom-call(f32[512,128]{1,0:T(8,128)S(1)} %bitcast.15, f32[4,256,128]{2,1,0:T(8,128)S(1)} %get-tuple-element.14.response, f32[512,256]{1,0:T(8,128)S(1)} %copy-done, f32[2,256,128]{2,1,0:T(8,128)S(1)} %copy-done.1, f32[256,256]{1,0:T(8,128)S(1)} %copy-done.2, f32[256,256]{1,0:T(8,128)S(1)} %copy-done.3), custom_call_target="tpu_custom_call" | custom-call | tf_op jit(solution)/shard_map/pallas_call | solution.py:80
  118.8 5.9 %all-to-all-start.4 = ((s32[256,2,128]{2,1,0:T(2,128)}), s32[256,2,128]{2,1,0:T(2,128)S(1)}, u32[]{:S(2)}, u32[]{:S(2)}) async-start(s32[256,2,128]{2,1,0:T(2,128)} %bitcast.7), calls=%async_computation.4 | async-start | bytes 524288 | tf_op jit(solution)/shard_map/all_to_all | solution.py:446
  124.7 1.7 %collective-permute-start = (f32[32,128]{1,0:T(8,128)S(1)}, f32[32,128]{1,0:T(8,128)S(1)}, u32[]{:S(2)}, u32[]{:S(2)}) collective-permute-start(f32[32,128]{1,0:T(8,128)S(1)} %get-tuple-element.18), channel_id=1, source_target_pairs={{0,1},{1,2},{2,3},{3,4},{4,5},{5,6},{6,7},{7,8},{8,9},{9,10},{10,1... | collective-permute-start | bytes 49160 | tf_op jit(solution)/shard_map/ppermute | solution.py:502
  126.4 0.7 collective-permute-start.1
  127.7 2.2 %collective-permute-done.1.below = f32[32,128]{1,0:T(8,128)S(1)} collective-permute-done((f32[32,128]{1,0:T(8,128)S(1)}, f32[32,128]{1,0:T(8,128)S(1)}, u32[]{:S(2)}, u32[]{:S(2)}) %collective-permute-start.1) | collective-permute-done | bytes 16416 | tf_op jit(solution)/shard_map/ppermute | solution.py:503
  130.2 9.9 %all-to-all-done.4 = s32[256,2,128]{2,1,0:T(2,128)S(1)} async-done(((s32[256,2,128]{2,1,0:T(2,128)}), s32[256,2,128]{2,1,0:T(2,128)S(1)}, u32[]{:S(2)}, u32[]{:S(2)}) %all-to-all-start.4) | async-done | bytes 262176 | tf_op jit(solution)/shard_map/all_to_all | solution.py:446
  140.0 1.2 shard_map.183
  141.2 12.9 %all_to_all.33 = f32[32,16,128]{2,1,0:T(8,128)S(1)} all-to-all(f32[32,16,128]{2,1,0:T(8,128)S(1)} %shard_map.183), channel_id=1, replica_groups=mesh['sy'=8,'sx'=32] {'sx'}, dimensions={0} | all-to-all | bytes 524288 | tf_op jit(solution)/shard_map/all_to_all | solution.py:446
  154.2 0.7 slice_bitcast_fusion
  (32 shorter events, 1.8 us)
Async XLA Ops:
  0.6 0.7 copy-start.15
  1.3 0.9 copy-start.9
  2.2 0.9 copy-start.10
  3.1 0.9 copy-start.11
  4.0 0.9 copy-start.12
  4.9 11.1 %copy-start.5 = (f32[4,2,8,4096]{3,2,1,0:T(8,128)S(1)}, f32[4,2,8,4096]{3,2,1,0:T(8,128)}, u32[]{:S(2)}) copy-start(f32[4,2,8,4096]{3,2,1,0:T(8,128)} %transfer.1) | copy-start | bytes 3145732
  6.4 9.6 %copy-start.14 = (f32[2,128,128]{2,1,0:T(8,128)S(1)}, f32[2,128,128]{2,1,0:T(8,128)}, u32[]{:S(2)}) copy-start(f32[2,128,128]{2,1,0:T(8,128)} %constant.58.clone.flips) | copy-start | bytes 393220
  6.4 21.6 %all-to-all-start = ((bf16[32,80,128]{2,1,0:T(8,128)(2,1)}), bf16[32,80,128]{2,1,0:T(8,128)(2,1)S(1)}, u32[]{:S(2)}, u32[]{:S(2)}) async-start(bf16[32,80,128]{2,1,0:T(8,128)(2,1)} %shard_map.176), calls=%async_computation | async-start | bytes 1310720 | tf_op jit(solution)/shard_map/all_to_all | solution.py:446
  16.1 12.0 %copy-start.6 = (f32[256,256]{1,0:T(8,128)S(1)}, f32[256,256]{1,0:T(8,128)}, u32[]{:S(2)}) copy-start(f32[256,256]{1,0:T(8,128)} %constant.52.clone.matrix.forward) | copy-start | bytes 786436
  16.1 12.0 %copy-start.7 = (f32[2,32,128]{2,1,0:T(8,128)S(1)}, f32[2,32,128]{2,1,0:T(8,128)}, u32[]{:S(2)}) copy-start(f32[2,32,128]{2,1,0:T(8,128)} %constant.51.clone.turn) | copy-start | bytes 98308
  28.0 37.7 %copy-start.13 = (f32[2,128,128]{2,1,0:T(8,128)S(1)}, f32[2,128,128]{2,1,0:T(8,128)}, u32[]{:S(2)}) copy-start(f32[2,128,128]{2,1,0:T(8,128)} %constant.60.clone.flip_lams) | copy-start | bytes 393220
  30.1 35.7 %copy-start = (f32[512,256]{1,0:T(8,128)S(1)}, f32[512,256]{1,0:T(8,128)}, u32[]{:S(2)}) copy-start(f32[512,256]{1,0:T(8,128)} %constant.54.clone.y_long) | copy-start | bytes 1572868
  30.1 35.7 %copy-start.1 = (f32[2,256,128]{2,1,0:T(8,128)S(1)}, f32[2,256,128]{2,1,0:T(8,128)}, u32[]{:S(2)}) copy-start(f32[2,256,128]{2,1,0:T(8,128)} %constant.55.clone.turn_y) | copy-start | bytes 786436
  30.1 35.7 %copy-start.2 = (f32[256,256]{1,0:T(8,128)S(1)}, f32[256,256]{1,0:T(8,128)}, u32[]{:S(2)}) copy-start(f32[256,256]{1,0:T(8,128)} %constant.56.clone.forward) | copy-start | bytes 786436
  30.1 35.7 %copy-start.3 = (f32[256,256]{1,0:T(8,128)S(1)}, f32[256,256]{1,0:T(8,128)}, u32[]{:S(2)}) copy-start(f32[256,256]{1,0:T(8,128)} %constant.57.clone.inverse) | copy-start | bytes 786436
  30.1 35.7 %copy-start.8 = (f32[256,256]{1,0:T(8,128)S(1)}, f32[256,256]{1,0:T(8,128)}, u32[]{:S(2)}) copy-start(f32[256,256]{1,0:T(8,128)} %constant.59.clone.flip_rows) | copy-start | bytes 786436
  70.7 21.6 %copy-start.4 = (f32[256,256]{1,0:T(8,128)S(1)}, f32[256,256]{1,0:T(8,128)}, u32[]{:S(2)}) copy-start(f32[256,256]{1,0:T(8,128)} %constant.53.clone.inverse) | copy-start | bytes 786436
  118.8 21.3 %all-to-all-start.4 = ((s32[256,2,128]{2,1,0:T(2,128)}), s32[256,2,128]{2,1,0:T(2,128)S(1)}, u32[]{:S(2)}, u32[]{:S(2)}) async-start(s32[256,2,128]{2,1,0:T(2,128)} %bitcast.7), calls=%async_computation.4 | async-start | bytes 524288 | tf_op jit(solution)/shard_map/all_to_all | solution.py:446
  124.7 3.0 %collective-permute-start = (f32[32,128]{1,0:T(8,128)S(1)}, f32[32,128]{1,0:T(8,128)S(1)}, u32[]{:S(2)}, u32[]{:S(2)}) collective-permute-start(f32[32,128]{1,0:T(8,128)S(1)} %get-tuple-element.18), channel_id=1, source_target_pairs={{0,1},{1,2},{2,3},{3,4},{4,5},{5,6},{6,7},{7,8},{8,9},{9,10},{10,1... | collective-permute-start | bytes 49160 | tf_op jit(solution)/shard_map/ppermute | solution.py:502
  126.4 3.5 %collective-permute-start.1 = (f32[32,128]{1,0:T(8,128)S(1)}, f32[32,128]{1,0:T(8,128)S(1)}, u32[]{:S(2)}, u32[]{:S(2)}) collective-permute-start(f32[32,128]{1,0:T(8,128)S(1)} %get-tuple-element.19), channel_id=1, source_target_pairs={{1,0},{2,1},{3,2},{4,3},{5,4},{6,5},{7,6},{8,7},{9,8},{10,9},{11,1... | collective-permute-start | bytes 49160 | tf_op jit(solution)/shard_map/ppermute | solution.py:503

commit v3 on v2

--- a/solution.py
+++ b/solution.py
@@ -24,13 +24,29 @@
     return np.asarray(array, np.float32)
 
 
+def parts_of(array):
+    exact = np.asarray(array, np.float32)
+    high = exact.astype(jnp.bfloat16)
+    return high, (exact - high.astype(np.float32)).astype(jnp.bfloat16)
+
+
+def on_left(array):
+    high, low = parts_of(array)
+    return np.concatenate([high, high, low], axis=1)
+
+
+def on_right(array):
+    high, low = parts_of(array)
+    return np.concatenate([high, high, low], axis=0)
+
+
 def circle(left, right, length):
     angles = np.outer(np.arange(left), np.arange(right)) % length * (2.0 * np.pi / length)
     return np.cos(angles), np.sin(angles)
 
 
 def joined(cos, sin, sign):
-    return table(np.block([[cos, sign * sin], [-sign * sin, cos]]))
+    return on_right(np.block([[cos, sign * sin], [-sign * sin, cos]]))
 
 
 def make_tables():
@@ -58,15 +74,17 @@
         turn_x=table(np.stack([cos_turn, sin_turn])),
         x_forward=joined(cos_long, sin_long, -1.0),
         x_inverse=joined(cos_long, sin_long, 1.0),
-        y_long=table(np.concatenate([cos_dev, sin_dev])),
+        y_long=on_left(np.concatenate([cos_dev, sin_dev])),
         turn_y=table(
             np.stack([np.repeat(cos_row, PIECE, axis=1), np.repeat(sin_row, PIECE, axis=1)])
         ),
         y_forward=joined(wide(cos_eight), wide(sin_eight), -1.0),
         y_inverse=joined(wide(cos_eight), wide(sin_eight), 1.0),
         flips=table(np.stack([flip, flip_first])),
-        flip_rows=table(flip_rows),
-        flip_lams=table(np.stack([wide(flip_lam), wide(flip_lam_first)])),
+        flip_rows=np.tile(flip_rows, (1, 2)).astype(jnp.bfloat16),
+        flip_lams=np.stack(
+            [np.tile(wide(flip), (2, 1)) for flip in (flip_lam, flip_lam_first)]
+        ).astype(jnp.bfloat16),
     )
 
 
@@ -74,14 +92,38 @@
     return jnp.dot(left, right, precision=highest, preferred_element_type=f32)
 
 
-def run(body, shapes, *operands, scalars=0, scratch=()):
+def split(value):
+    high = value.astype(jnp.bfloat16)
+    return high, (value - high.astype(f32)).astype(jnp.bfloat16)
+
+
+def product(left, right):
+    return jnp.dot(left, right, preferred_element_type=f32)
+
+
+def times_left(factor, value):
+    high, low = split(value)
+    return product(factor[...], jnp.concatenate([high, low, high], axis=0))
+
+
+def times_right(value, factor):
+    high, low = split(value)
+    return product(jnp.concatenate([high, low, high], axis=1), factor[...])
+
+
+def run(body, shapes, *operands, scalars=0, far=0, scratch=()):
     whole = pl.BlockSpec(memory_space=pltpu.VMEM)
+    operands = [
+        pltpu.with_memory_space_constraint(operand, pltpu.HBM) if n < far else operand
+        for n, operand in enumerate(operands)
+    ]
     single = not isinstance(shapes, (list, tuple))
     return pl.pallas_call(
         body,
         out_shape=shapes,
         in_specs=[pl.BlockSpec(memory_space=pltpu.SMEM)] * scalars
-        + [whole] * (len(operands) - scalars),
+        + [pl.BlockSpec(memory_space=pltpu.HBM)] * far
+        + [whole] * (len(operands) - scalars - far),
         out_specs=whole if single else [whole] * len(shapes),
         scratch_shapes=list(scratch),
         compiler_params=pltpu.CompilerParams(vmem_limit_bytes=48 * 1024 * 1024),
@@ -190,18 +232,41 @@
     ]
 
 
+def low_half(field):
+    return lax.broadcasted_iota(jnp.int32, field.shape, 1) < field.shape[1] // 2
+
+
+def paired(field):
+    other = pltpu.roll(field, field.shape[1] // 2, 1)
+    low = low_half(field)
+    return jnp.where(low, field, other), jnp.where(low, other, field)
+
+
+def encode_pair(real, imag):
+    first_real, second_real = paired(real)
+    first_imag, second_imag = paired(imag)
+    words = encode([first_real, first_imag, second_real, second_imag])
+    return jnp.where(low_half(real), *words)
+
+
+def decode_pair(word):
+    values = decode(*paired(word))
+    low = low_half(word)
+    return jnp.where(low, values[0], values[2]), jnp.where(low, values[1], values[3])
+
+
 def rows_to_lines(points, turn, matrix, work):
     for c, (real, imag) in enumerate(short_transform(points, -1.0)):
         cos, sin = turn[0, c : c + 1, :], turn[1, c : c + 1, :]
         imag = jnp.zeros_like(real) if imag is None else imag
         work[ROWS * c : ROWS * (c + 1), :LANES] = real * cos + imag * sin
         work[ROWS * c : ROWS * (c + 1), LANES:] = imag * cos - real * sin
-    lines = dot(work[...], matrix[...])
+    lines = times_right(work[...], matrix)
     return [lines[:, :LANES], lines[:, LANES:]]
 
 
 def lines_to_rows(real, imag, turn, matrix, work):
-    work[...] = dot(jnp.concatenate([real, imag], axis=1), matrix[...])
+    work[...] = times_right(jnp.concatenate([real, imag], axis=1), matrix)
     points = []
     for c in range(SHORT):
         cos, sin = turn[0, c : c + 1, :], turn[1, c : c + 1, :]
@@ -212,7 +277,7 @@
 
 
 def forward_y(received, y_long, turn_y, matrix):
-    both = dot(y_long[...], jnp.concatenate(received, axis=1))
+    both = times_left(y_long, jnp.concatenate(received, axis=1))
     by_cos, by_sin = both[:DEVICES], both[DEVICES:]
     cos, sin = turn_y[0], turn_y[1]
     spectra = []
@@ -222,7 +287,7 @@
         real = by_cos[:, at_real] + by_sin[:, at_imag]
         imag = by_cos[:, at_imag] - by_sin[:, at_real]
         lines = jnp.concatenate([real * cos + imag * sin, imag * cos - real * sin], axis=1)
-        out = dot(lines, matrix[...])
+        out = times_right(lines, matrix)
         spectra.append((out[:, :LANES], out[:, LANES:]))
     return spectra
 
@@ -231,10 +296,10 @@
     cos, sin = turn_y[0], turn_y[1]
     columns = []
     for real, imag in spectra:
-        lines = dot(jnp.concatenate([real, imag], axis=1), matrix[...])
+        lines = times_right(jnp.concatenate([real, imag], axis=1), matrix)
         real, imag = lines[:, :LANES], lines[:, LANES:]
         columns += [real * cos - imag * sin, real * sin + imag * cos]
-    both = dot(y_long[...], jnp.concatenate(columns, axis=1))
+    both = times_left(y_long, jnp.concatenate(columns, axis=1))
     by_cos, by_sin = both[:DEVICES], both[DEVICES:]
     fields = []
     for f in range(0, len(columns), 2):
@@ -265,7 +330,16 @@
     return both[:ROWS] + both[ROWS:]
 
 
-def pack_inputs(counts, tiles, sky, observed, noise, sent):
+def pack_inputs(*refs):
+    sources, sent, held, done = refs[:5], refs[5], refs[6:11], refs[11]
+    copies = [
+        pltpu.make_async_copy(source, target, done.at[n])
+        for n, (source, target) in enumerate(zip(sources, held))
+    ]
+    for copy in copies:
+        copy.start()
+    tiles, counts, *fields = held
+    copies[0].wait()
     for piece in range(PIECE):
         rows = jnp.concatenate(
             [
@@ -276,13 +350,15 @@
         ).astype(jnp.bfloat16)
         sent[piece, :TILE_ROWS, :] = rows
         sent[piece + PIECE, :TILE_ROWS, :] = rows
+    copies[1].wait()
     lane = lax.broadcasted_iota(jnp.int32, (ROWS, LANES), 1)
-    for r in range(SHORT):
-        rows = slice(ROWS * r, ROWS * (r + 1))
-        weight = noise[rows, :]
-        weight = jnp.where(lane < counts[r // PIECE], -weight, weight)
-        for f, value in enumerate((sky[rows, :], observed[rows, :], weight)):
-            start = TILE_ROWS + 2 * ROWS * f
+    for f, field in enumerate(fields):
+        copies[2 + f].wait()
+        start = TILE_ROWS + 2 * ROWS * f
+        for r in range(SHORT):
+            value = field[ROWS * r : ROWS * (r + 1), :]
+            if f == 2:
+                value = jnp.where(lane < counts[r // PIECE], -value, value)
             sent[r, start : start + 2 * ROWS, :] = halves(value)
 
 
@@ -325,26 +401,25 @@
         c_real, c_imag = response[2 * p], response[2 * p + 1]
         real = real + z_real * c_real - z_imag * c_imag
         imag = imag + z_real * c_imag + z_imag * c_real
-    put(sent, inverse_y([(real, imag)], y_long, turn_y, inverse), 0, 2)
+    sent[...] = encode_pair(*inverse_y([(real, imag)], y_long, turn_y, inverse))
 
 
 def middle_rows(received, parts, turn, forward, inverse, sent, residual, work):
-    points = lines_to_rows(
-        swapped(every(received, 0, 2)), swapped(every(received, 1, 2)), turn, inverse, work
-    )
+    word = swap_blocks(received[...].reshape(SHORT, ROWS, LANES))
+    real, imag = (part.reshape(DEVICES, LANES) for part in decode_pair(word))
+    points = lines_to_rows(real, imag, turn, inverse, work)
     values = []
     for b in range(SHORT):
         value = jnp.abs(pixel(parts, b, 2)) * (points[b][0] - pixel(parts, b, 1))
         residual[b] = value
         values.append((value, None))
     fields = rows_to_lines(values, turn, forward, work)
-    put(sent, [swapped(field) for field in fields], 0, 2)
+    word = encode_pair(*(field.reshape(SHORT, ROWS, LANES) for field in fields))
+    sent[...] = swap_blocks(word).reshape(DEVICES, LANES)
 
 
 def last_lines(received, response, y_long, turn_y, forward, inverse, sent):
-    ((real, imag),) = forward_y(
-        [every(received, 0, 2), every(received, 1, 2)], y_long, turn_y, forward
-    )
+    ((real, imag),) = forward_y(decode_pair(received[...]), y_long, turn_y, forward)
     spectra = []
     for p in range(2):
         c_real, c_imag = response[2 * p], response[2 * p + 1]
@@ -429,13 +504,14 @@
             for v in range(PIECE):
                 fields[w, pl.ds(LANES * low + v, ROWS, stride=PIECE), :] = word[PIECE * low + v]
     direct = decode(fields[0], fields[1])
-    mirror = dot(flip_rows[...], jnp.concatenate(decode(fields[2], fields[3]), axis=1))
+    high, low = split(jnp.concatenate(decode(fields[2], fields[3]), axis=1))
+    mirror = product(flip_rows[...], jnp.concatenate([high, low], axis=0))
     scale = f32(0.5 / (NX * NY))
     top = lax.broadcasted_iota(jnp.int32, (DEVICES, LANES), 0) == 0
     for f in range(4):
-        lines = mirror[:, f * LANES : (f + 1) * LANES]
-        first = dot(lines[0:ROWS], flip_lams[1])
-        lines = dot(lines, flip_lams[0])
+        lines = jnp.concatenate(split(mirror[:, f * LANES : (f + 1) * LANES]), axis=1)
+        first = product(lines[0 : 2 * ROWS], flip_lams[1])
+        lines = product(lines, flip_lams[0])
         lines = jnp.where(top, jnp.broadcast_to(first[0:1], lines.shape), lines)
         response[f] = (direct[f] + lines if f % 2 == 0 else direct[f] - lines) * scale
 
@@ -460,12 +536,18 @@
         run(
             pack_inputs,
             shaped(SHORT, TILE_ROWS + 6 * ROWS, LANES, dtype=jnp.bfloat16),
+            basis_tiles,
             counts.reshape(2),
-            basis_tiles,
             sky_image,
             observed,
             noise_weight,
-            scalars=1,
+            far=5,
+            scratch=[
+                pltpu.VMEM(basis_tiles.shape, basis_tiles.dtype),
+                pltpu.SMEM((2,), jnp.int32),
+            ]
+            + [pltpu.VMEM(sky_image.shape, f32)] * 3
+            + [pltpu.SemaphoreType.DMA((5,))],
         ),
         "sx",
         SHORT,
@@ -506,7 +588,7 @@
     x_tables = [tables[name] for name in ("turn_x", "x_forward", "x_inverse")]
     sent, response = run(
         middle_lines,
-        [shaped(DEVICES * 2, LANES), shaped(4, DEVICES, LANES)],
+        [shaped(DEVICES, LANES, dtype=jnp.int32), shaped(4, DEVICES, LANES)],
         received,
         tables["flip_rows"],
         tables["flip_lams"],
@@ -516,7 +598,7 @@
     received = exchange(sent, EVERY, DEVICES)
     sent, residual = run(
         middle_rows,
-        [shaped(DEVICES * 2, LANES), shaped(SHORT, ROWS, LANES)],
+        [shaped(DEVICES, LANES, dtype=jnp.int32), shaped(SHORT, ROWS, LANES)],
         received,
         parts,
         *x_tables,

time: 155 us -> 142 us (0.916)
  blocking collectives: 91 us -> 86.1 us
  local copies, waits for them, and re-layouts: 5.24 us -> 0.98 us
  Pallas kernels: 16.9 us -> 13.3 us
    all_to_all x4, blocking collectives: 91 us -> 86.1 us  [exchange(): lax.all_to_all(sent.reshape(shape), axis, split_axis=0, concat_axis=0, ti...]
    unnamed x32 -> x22, local copies, waits for them, and re-layouts: 4.33 us -> 0.07 us
    pallas_call x8, Pallas kernels: 16.9 us -> 13.3 us  [run(): pl.pallas_call(body, out_shape=shapes, in_specs=[pl.BlockSpec(memory_spac...]
where the time goes in v3:
time: 142 us
  blocking collectives  86.1 us (61%)
  waiting for transfers between devices  23.2 us (16%)
  starting transfers between devices  16.7 us (12%)
  Pallas kernels  13.3 us (9%)
    all_to_all x4, blocking collectives, exchange(): lax.all_to_all(sent.reshape(shape), axis, split_axis=0, concat_axis=0, ti...  86.1 us
    all_to_all x2, waiting for transfers between devices, exchange(): lax.all_to_all(sent.reshape(shape), axis, split_axis=0, concat_axis=0, ti...  20.4 us
    all_to_all x2, starting transfers between devices, exchange(): lax.all_to_all(sent.reshape(shape), axis, split_axis=0, concat_axis=0, ti...  14.3 us
    pallas_call x8, Pallas kernels, run(): pl.pallas_call(body, out_shape=shapes, in_specs=[pl.BlockSpec(memory_spac...  13.3 us
  transfers between devices with their start and end apart: 4, of which 4 were waited for; matrix products, arithmetic and copies ran while one was open for 1% of the time, Pallas kernels for 1%

profile of v3, /device:TPU:1, one launch (start us, length us, event | category | flops | bytes accessed | tf_op | source)
XLA Modules:
  0.0 141.8 jit_solution(15718741691684546202)
XLA Ops:
  0.6 2.1 %shard_map.176 = bf16[32,80,128]{2,1,0:T(8,128)(2,1)} custom-call(bf16[4,128,128]{2,1,0:T(8,128)(2,1)} %refs_0_.1, s32[2]{0:T(128)} %bitcast.24, f32[256,128]{1,0:T(8,128)} %refs_2_.1, f32[256,128]{1,0:T(8,128)} %refs_3_.1, f32[256,128]{1,0:T(8,128)} %refs_4_.1), custom_call_target="tpu_custom_call" | custom-call | tf_op jit(solution)/shard_map/pallas_call | solution.py:121
  2.8 8.7 %all-to-all-start = ((bf16[32,80,128]{2,1,0:T(8,128)(2,1)}), bf16[32,80,128]{2,1,0:T(8,128)(2,1)S(1)}, u32[]{:S(2)}, u32[]{:S(2)}) async-start(bf16[32,80,128]{2,1,0:T(8,128)(2,1)} %shard_map.176), calls=%async_computation | async-start | bytes 1310720 | tf_op jit(solution)/shard_map/all_to_all | solution.py:522
  11.5 0.7 dynamic-slice_subtract_fusion
  12.2 0.1 copy.21
  12.3 0.1 sub.15.wanted
  12.5 1.4 %shard_map.177.spread = s32[4,256,128]{2,1,0:T(8,128)S(1)} custom-call(f32[4,2,8,4096]{3,2,1,0:T(8,128)S(1)} %copy-done.5, f32[2,128,128]{2,1,0:T(8,128)S(1)} %copy-done.10), custom_call_target="tpu_custom_call" | custom-call | tf_op jit(solution)/shard_map/pallas_call | solution.py:121
  13.9 10.5 %all-to-all-done.parts = bf16[32,80,128]{2,1,0:T(8,128)(2,1)S(1)} async-done(((bf16[32,80,128]{2,1,0:T(8,128)(2,1)}), bf16[32,80,128]{2,1,0:T(8,128)(2,1)S(1)}, u32[]{:S(2)}, u32[]{:S(2)}) %all-to-all-start) | async-done | bytes 655392 | tf_op jit(solution)/shard_map/all_to_all | solution.py:522
  24.4 1.6 %shard_map.178 = (s32[1536,128]{1,0:T(8,128)S(1)}, f32[4,32,8,128]{3,2,1,0:T(8,128)S(1)}, f32[32,8,128]{2,1,0:T(8,128)S(1)}, f32[32,128]{1,0:T(8,128)S(1)}, f32[32,128]{1,0:T(8,128)S(1)}) custom-call(s32[128]{0:T(128)S(1)} %sub.15.wanted, bf16[32,80,128]{2,1,0:T(8,128)(2,1)S(1)} %all-to-all-done.parts, s32[4,256,128]{2,1,0:T(8,128)S(1)} %shard_map.177.spread, ...), custom_call_target="tpu_custom_call" | custom-call | tf_op jit(solution)/shard_map/pallas_call | solution.py:121
  26.1 35.7 %all_to_all.30 = s32[256,1,768]{2,1,0:T(1,128)S(1)} all-to-all(s32[256,1,768]{2,1,0:T(1,128)S(1)} %bitcast.19), channel_id=1, replica_groups=mesh['sy'=8,'sx'=32] {'sy','sx'}, dimensions={0} | all-to-all | bytes 1572864 | tf_op jit(solution)/shard_map/all_to_all | solution.py:522
  61.9 2.9 %shard_map.179 = (s32[256,128]{1,0:T(8,128)S(1)}, f32[4,256,128]{2,1,0:T(8,128)S(1)}) custom-call(s32[1536,128]{1,0:T(8,128)S(1)} %bitcast.17, bf16[256,512]{1,0:T(8,128)(2,1)S(1)} %copy-done.8, bf16[2,256,128]{2,1,0:T(8,128)(2,1)S(1)} %copy-done.9, bf16[512,768]{1,0:T(8,128)(2,1)S(1)} %copy-done, f32[2,256,128]{2,1,0:T(8,128)S(1)} %copy-done.6, ...), custom_call_target="tpu_custom_call" | custom-call | tf_op jit(solution)/shard_map/pallas_call | solution.py:121
  64.7 19.2 %all_to_all.31 = s32[256,1,128]{2,1,0:T(1,128)S(1)} all-to-all(s32[256,1,128]{2,1,0:T(1,128)S(1)} %bitcast.22), channel_id=1, replica_groups=mesh['sy'=8,'sx'=32] {'sy','sx'}, dimensions={0} | all-to-all | bytes 262144 | tf_op jit(solution)/shard_map/all_to_all | solution.py:522
  83.9 1.4 %shard_map.180 = (s32[256,128]{1,0:T(8,128)S(1)}, f32[32,8,128]{2,1,0:T(8,128)S(1)}) custom-call(s32[256,128]{1,0:T(8,128)S(1)} %bitcast.20, bf16[32,80,128]{2,1,0:T(8,128)(2,1)S(1)} %all-to-all-done.parts, f32[2,32,128]{2,1,0:T(8,128)S(1)} %copy-done.7, bf16[768,256]{1,0:T(8,128)(2,1)S(1)} %copy-done.2, bf16[768,256]{1,0:T(8,128)(2,1)S(1)} %copy-done.1), custom_call_target="tpu_custom_call" | custom-call | tf_op jit(solution)/shard_map/pallas_call | solution.py:121
  85.4 18.4 %all_to_all.32 = s32[256,1,128]{2,1,0:T(1,128)S(1)} all-to-all(s32[256,1,128]{2,1,0:T(1,128)S(1)} %bitcast.23), channel_id=1, replica_groups=mesh['sy'=8,'sx'=32] {'sy','sx'}, dimensions={0} | all-to-all | bytes 262144 | tf_op jit(solution)/shard_map/all_to_all | solution.py:522
  103.7 2.6 %shard_map.181 = s32[512,128]{1,0:T(8,128)} custom-call(s32[256,128]{1,0:T(8,128)S(1)} %bitcast.21, f32[4,256,128]{2,1,0:T(8,128)S(1)} %get-tuple-element.14.response, bf16[512,768]{1,0:T(8,128)(2,1)S(1)} %copy-done, f32[2,256,128]{2,1,0:T(8,128)S(1)} %copy-done.6, bf16[768,256]{1,0:T(8,128)(2,1)S(1)} %copy-done.3, bf16[768,256]{1,0:T(8,128)(2,1)S(1)} %copy-done.4), custom_call_target="tpu_custom_call" | custom-call | tf_op jit(solution)/shard_map/pallas_call | solution.py:121
  106.3 5.5 %all-to-all-start.4 = ((s32[256,2,128]{2,1,0:T(2,128)}), s32[256,2,128]{2,1,0:T(2,128)S(1)}, u32[]{:S(2)}, u32[]{:S(2)}) async-start(s32[256,2,128]{2,1,0:T(2,128)} %bitcast.9), calls=%async_computation.4 | async-start | bytes 524288 | tf_op jit(solution)/shard_map/all_to_all | solution.py:522
  111.9 1.7 %collective-permute-start = (f32[32,128]{1,0:T(8,128)S(1)}, f32[32,128]{1,0:T(8,128)S(1)}, u32[]{:S(2)}, u32[]{:S(2)}) collective-permute-start(f32[32,128]{1,0:T(8,128)S(1)} %get-tuple-element.18), channel_id=1, source_target_pairs={{0,1},{1,2},{2,3},{3,4},{4,5},{5,6},{6,7},{7,8},{8,9},{9,10},{10,1... | collective-permute-start | bytes 49160 | tf_op jit(solution)/shard_map/ppermute | solution.py:584
  113.6 0.7 collective-permute-start.1
  114.3 0.6 collective-permute-done.above
  114.9 2.2 %collective-permute-done.1.below = f32[32,128]{1,0:T(8,128)S(1)} collective-permute-done((f32[32,128]{1,0:T(8,128)S(1)}, f32[32,128]{1,0:T(8,128)S(1)}, u32[]{:S(2)}, u32[]{:S(2)}) %collective-permute-start.1) | collective-permute-done | bytes 16416 | tf_op jit(solution)/shard_map/ppermute | solution.py:585
  117.1 0.3 shard_map.182.flow
  117.4 9.9 %all-to-all-done.4 = s32[256,2,128]{2,1,0:T(2,128)S(1)} async-done(((s32[256,2,128]{2,1,0:T(2,128)}), s32[256,2,128]{2,1,0:T(2,128)S(1)}, u32[]{:S(2)}, u32[]{:S(2)}) %all-to-all-start.4) | async-done | bytes 262176 | tf_op jit(solution)/shard_map/all_to_all | solution.py:522
  127.3 0.9 shard_map.183
  128.2 12.9 %all_to_all.33 = f32[32,16,128]{2,1,0:T(8,128)S(1)} all-to-all(f32[32,16,128]{2,1,0:T(8,128)S(1)} %shard_map.183), channel_id=1, replica_groups=mesh['sy'=8,'sx'=32] {'sx'}, dimensions={0} | all-to-all | bytes 524288 | tf_op jit(solution)/shard_map/all_to_all | solution.py:522
  141.1 0.7 slice_bitcast_fusion
  (22 shorter events, 0.1 us)
Async XLA Ops:
  0.6 11.8 %copy-start.5 = (f32[4,2,8,4096]{3,2,1,0:T(8,128)S(1)}, f32[4,2,8,4096]{3,2,1,0:T(8,128)}, u32[]{:S(2)}) copy-start(f32[4,2,8,4096]{3,2,1,0:T(8,128)} %transfer.1) | copy-start | bytes 3145732
  2.7 9.7 %copy-start.10 = (f32[2,128,128]{2,1,0:T(8,128)S(1)}, f32[2,128,128]{2,1,0:T(8,128)}, u32[]{:S(2)}) copy-start(f32[2,128,128]{2,1,0:T(8,128)} %constant.58.clone.flips) | copy-start | bytes 393220
  2.8 21.6 %all-to-all-start = ((bf16[32,80,128]{2,1,0:T(8,128)(2,1)}), bf16[32,80,128]{2,1,0:T(8,128)(2,1)S(1)}, u32[]{:S(2)}, u32[]{:S(2)}) async-start(bf16[32,80,128]{2,1,0:T(8,128)(2,1)} %shard_map.176), calls=%async_computation | async-start | bytes 1310720 | tf_op jit(solution)/shard_map/all_to_all | solution.py:522
  12.4 12.0 %copy-start.2 = (bf16[768,256]{1,0:T(8,128)(2,1)S(1)}, bf16[768,256]{1,0:T(8,128)(2,1)}, u32[]{:S(2)}) copy-start(bf16[768,256]{1,0:T(8,128)(2,1)} %constant.52.clone.matrix.forward) | copy-start | bytes 1179652
  12.4 12.0 %copy-start.7 = (f32[2,32,128]{2,1,0:T(8,128)S(1)}, f32[2,32,128]{2,1,0:T(8,128)}, u32[]{:S(2)}) copy-start(f32[2,32,128]{2,1,0:T(8,128)} %constant.51.clone.turn) | copy-start | bytes 98308
  24.4 37.4 %copy-start.6 = (f32[2,256,128]{2,1,0:T(8,128)S(1)}, f32[2,256,128]{2,1,0:T(8,128)}, u32[]{:S(2)}) copy-start(f32[2,256,128]{2,1,0:T(8,128)} %constant.55.clone.turn_y) | copy-start | bytes 786436
  24.4 37.4 %copy-start.8 = (bf16[256,512]{1,0:T(8,128)(2,1)S(1)}, bf16[256,512]{1,0:T(8,128)(2,1)}, u32[]{:S(2)}) copy-start(bf16[256,512]{1,0:T(8,128)(2,1)} %constant.59.clone.flip_rows) | copy-start | bytes 786436
  24.4 37.4 %copy-start.9 = (bf16[2,256,128]{2,1,0:T(8,128)(2,1)S(1)}, bf16[2,256,128]{2,1,0:T(8,128)(2,1)}, u32[]{:S(2)}) copy-start(bf16[2,256,128]{2,1,0:T(8,128)(2,1)} %constant.60.clone.flip_lams) | copy-start | bytes 393220
  26.1 35.7 %copy-start = (bf16[512,768]{1,0:T(8,128)(2,1)S(1)}, bf16[512,768]{1,0:T(8,128)(2,1)}, u32[]{:S(2)}) copy-start(bf16[512,768]{1,0:T(8,128)(2,1)} %constant.54.clone.y_long) | copy-start | bytes 2359300
  26.1 35.7 %copy-start.3 = (bf16[768,256]{1,0:T(8,128)(2,1)S(1)}, bf16[768,256]{1,0:T(8,128)(2,1)}, u32[]{:S(2)}) copy-start(bf16[768,256]{1,0:T(8,128)(2,1)} %constant.56.clone.forward) | copy-start | bytes 1179652
  26.1 35.7 %copy-start.4 = (bf16[768,256]{1,0:T(8,128)(2,1)S(1)}, bf16[768,256]{1,0:T(8,128)(2,1)}, u32[]{:S(2)}) copy-start(bf16[768,256]{1,0:T(8,128)(2,1)} %constant.57.clone.inverse) | copy-start | bytes 1179652
  61.8 22.1 %copy-start.1 = (bf16[768,256]{1,0:T(8,128)(2,1)S(1)}, bf16[768,256]{1,0:T(8,128)(2,1)}, u32[]{:S(2)}) copy-start(bf16[768,256]{1,0:T(8,128)(2,1)} %constant.53.clone.inverse) | copy-start | bytes 1179652
  106.3 21.0 %all-to-all-start.4 = ((s32[256,2,128]{2,1,0:T(2,128)}), s32[256,2,128]{2,1,0:T(2,128)S(1)}, u32[]{:S(2)}, u32[]{:S(2)}) async-start(s32[256,2,128]{2,1,0:T(2,128)} %bitcast.9), calls=%async_computation.4 | async-start | bytes 524288 | tf_op jit(solution)/shard_map/all_to_all | solution.py:522
  111.9 3.0 %collective-permute-start = (f32[32,128]{1,0:T(8,128)S(1)}, f32[32,128]{1,0:T(8,128)S(1)}, u32[]{:S(2)}, u32[]{:S(2)}) collective-permute-start(f32[32,128]{1,0:T(8,128)S(1)} %get-tuple-element.18), channel_id=1, source_target_pairs={{0,1},{1,2},{2,3},{3,4},{4,5},{5,6},{6,7},{7,8},{8,9},{9,10},{10,1... | collective-permute-start | bytes 49160 | tf_op jit(solution)/shard_map/ppermute | solution.py:584
  113.6 3.5 %collective-permute-start.1 = (f32[32,128]{1,0:T(8,128)S(1)}, f32[32,128]{1,0:T(8,128)S(1)}, u32[]{:S(2)}, u32[]{:S(2)}) collective-permute-start(f32[32,128]{1,0:T(8,128)S(1)} %get-tuple-element.19), channel_id=1, source_target_pairs={{1,0},{2,1},{3,2},{4,3},{5,4},{6,5},{7,6},{8,7},{9,8},{10,9},{11,1... | collective-permute-start | bytes 49160 | tf_op jit(solution)/shard_map/ppermute | solution.py:585

commit v4 on v3

--- a/solution.py
+++ b/solution.py
@@ -8,7 +8,6 @@
 from jax.experimental.pallas import tpu as pltpu
 from jax.sharding import PartitionSpec as P
 
-highest = lax.Precision.HIGHEST
 tv_weight = 0.5
 smoothing = 0.25
 f32 = jnp.float32
@@ -58,18 +57,10 @@
     spread = np.eye(PIECE)
     wide = lambda matrix: np.kron(matrix, spread)
     lane = np.arange(LANES)
-    kappa = np.arange(DEVICES)
     flip = np.zeros((LANES, LANES))
     flip[LANES - 1 - lane, lane] = 1.0
     flip_first = np.zeros((LANES, LANES))
     flip_first[(LANES - lane) % LANES, lane] = 1.0
-    flip_rows = np.zeros((DEVICES, DEVICES))
-    flip_rows[kappa, (DEVICES - kappa) % DEVICES] = 1.0
-    lam = np.arange(ROWS)
-    flip_lam = np.zeros((ROWS, ROWS))
-    flip_lam[ROWS - 1 - lam, lam] = 1.0
-    flip_lam_first = np.zeros((ROWS, ROWS))
-    flip_lam_first[(ROWS - lam) % ROWS, lam] = 1.0
     return dict(
         turn_x=table(np.stack([cos_turn, sin_turn])),
         x_forward=joined(cos_long, sin_long, -1.0),
@@ -80,16 +71,10 @@
         ),
         y_forward=joined(wide(cos_eight), wide(sin_eight), -1.0),
         y_inverse=joined(wide(cos_eight), wide(sin_eight), 1.0),
-        flips=table(np.stack([flip, flip_first])),
-        flip_rows=np.tile(flip_rows, (1, 2)).astype(jnp.bfloat16),
-        flip_lams=np.stack(
-            [np.tile(wide(flip), (2, 1)) for flip in (flip_lam, flip_lam_first)]
-        ).astype(jnp.bfloat16),
-    )
-
-
-def dot(left, right):
-    return jnp.dot(left, right, precision=highest, preferred_element_type=f32)
+        flips=np.stack([np.tile(part, (2, 1)) for part in (flip, flip_first)]).astype(
+            jnp.bfloat16
+        ),
+    )
 
 
 def split(value):
@@ -113,6 +98,7 @@
 
 def run(body, shapes, *operands, scalars=0, far=0, scratch=()):
     whole = pl.BlockSpec(memory_space=pltpu.VMEM)
+    outside = pl.BlockSpec(memory_space=pltpu.HBM)
     operands = [
         pltpu.with_memory_space_constraint(operand, pltpu.HBM) if n < far else operand
         for n, operand in enumerate(operands)
@@ -122,9 +108,9 @@
         body,
         out_shape=shapes,
         in_specs=[pl.BlockSpec(memory_space=pltpu.SMEM)] * scalars
-        + [pl.BlockSpec(memory_space=pltpu.HBM)] * far
+        + [outside] * far
         + [whole] * (len(operands) - scalars - far),
-        out_specs=whole if single else [whole] * len(shapes),
+        out_specs=outside if far else whole if single else [whole] * len(shapes),
         scratch_shapes=list(scratch),
         compiler_params=pltpu.CompilerParams(vmem_limit_bytes=48 * 1024 * 1024),
     )(*operands)
@@ -331,11 +317,18 @@
 
 
 def pack_inputs(*refs):
-    sources, sent, held, done = refs[:5], refs[5], refs[6:11], refs[11]
+    sources, target, held, sent, done, left = refs[:5], refs[5], refs[6:11], *refs[11:]
     copies = [
-        pltpu.make_async_copy(source, target, done.at[n])
-        for n, (source, target) in enumerate(zip(sources, held))
+        pltpu.make_async_copy(source, local, done.at[n])
+        for n, (source, local) in enumerate(zip(sources, held))
     ]
+
+    def leave(n, start, stop):
+        rows = (slice(None), slice(start, stop), slice(None))
+        copy = pltpu.make_async_copy(sent.at[rows], target.at[rows], left.at[n])
+        copy.start()
+        return copy
+
     for copy in copies:
         copy.start()
     tiles, counts, *fields = held
@@ -350,6 +343,7 @@
         ).astype(jnp.bfloat16)
         sent[piece, :TILE_ROWS, :] = rows
         sent[piece + PIECE, :TILE_ROWS, :] = rows
+    leaving = [leave(0, 0, TILE_ROWS)]
     copies[1].wait()
     lane = lax.broadcasted_iota(jnp.int32, (ROWS, LANES), 1)
     for f, field in enumerate(fields):
@@ -360,6 +354,9 @@
             if f == 2:
                 value = jnp.where(lane < counts[r // PIECE], -value, value)
             sent[r, start : start + 2 * ROWS, :] = halves(value)
+        leaving.append(leave(1 + f, start, start + 2 * ROWS))
+    for copy in leaving:
+        copy.wait()
 
 
 def first_rows(wanted, parts, spread, turn, matrix, sent, coef, pixels, top, bottom, pool, work):
@@ -389,10 +386,8 @@
     put(sent, [spread[word] for word in range(4)], 2, 6)
 
 
-def middle_lines(
-    received, flip_rows, flip_lams, y_long, turn_y, forward, inverse, sent, response, fields
-):
-    make_response(received, flip_rows, flip_lams, response, fields)
+def middle_lines(received, y_long, turn_y, forward, inverse, sent, response, fields):
+    make_response(received, response, fields)
     spectra = forward_y(
         decode(every(received, 0, 6), every(received, 1, 6)), y_long, turn_y, forward
     )
@@ -470,7 +465,16 @@
     flow[...] = -tv_weight * (flow_x - before_x + flow_y - before_y)
 
 
-def pack_transfer(transfer, flips, sent, mirrored):
+def reversed_rows(field):
+    sub = lax.broadcasted_iota(jnp.int32, field.shape, 1)
+    for step in (1, 2):
+        field = jnp.where(
+            (sub & step) == 0, pltpu.roll(field, ROWS - step, 1), pltpu.roll(field, step, 1)
+        )
+    return pltpu.roll(field, 4, 1)
+
+
+def pack_transfer(special, transfer, flips, sent, mirrored):
     for p in range(2):
         for c in range(SHORT):
             at = slice(LANES * c, LANES * (c + 1))
@@ -484,36 +488,46 @@
     direct, reverse = [], []
     for f in range(4):
         direct.append(mirrored[4 + f])
-        first = dot(mirrored[f, 0:ROWS, :], flips[1])
-        others = dot(mirrored[f], flips[0])
-        blocks = [first] + [others[ROWS * c : ROWS * (c + 1)] for c in range(SHORT - 1, 0, -1)]
+        first = product(jnp.concatenate(split(mirrored[f, 0 : 2 * ROWS, :]), axis=1), flips[1])
+        others = product(jnp.concatenate(split(mirrored[f]), axis=1), flips[0])
+        blocks = [first[:ROWS]]
+        blocks += [others[ROWS * c : ROWS * (c + 1)] for c in range(SHORT - 1, 0, -1)]
         reverse.append(jnp.concatenate(blocks, axis=0))
-    for w, word in enumerate(encode(direct) + encode(reverse)):
+    for w, word in enumerate(encode(direct)):
         sent[w] = swapped(word)
-
-
-def make_response(received, flip_rows, flip_lams, response, fields):
+    for w, word in enumerate(encode(reverse)):
+        word = reversed_rows(word.reshape(SHORT, ROWS, LANES))
+        word = jnp.where(special[0] == 1, pltpu.roll(word, 1, 1), word)
+        sent[2 + w] = swap_blocks(word).reshape(DEVICES, LANES)
+
+
+def mirrored_blocks(blocks):
+    flipped = reversed_rows(jnp.stack(blocks))
+    of = lambda low, v: flipped[PIECE * low + v : PIECE * low + v + 1]
+    head = lax.broadcasted_iota(jnp.int32, (1, ROWS, LANES), 2) < PIECE
+    ordered = []
+    for low in range(2):
+        own = pltpu.roll(of(0, 0), 1, 1) if low == 0 else of(1, 0)
+        ordered.append(jnp.where(head, own, of(1 - low, 0)))
+        ordered += [of(1 - low, PIECE - v) for v in range(1, PIECE)]
+    return jnp.concatenate(ordered, axis=0)
+
+
+def make_response(received, response, fields):
     for w in range(4):
         blocks = [
             received[pl.ds((PIECE * v + low) * 6 + 2 + w, ROWS, stride=12), :]
             for low in range(2)
             for v in range(PIECE)
         ]
-        word = swap_blocks(jnp.stack(blocks))
+        word = swap_blocks(jnp.stack(blocks) if w < 2 else mirrored_blocks(blocks))
         for low in range(2):
             for v in range(PIECE):
                 fields[w, pl.ds(LANES * low + v, ROWS, stride=PIECE), :] = word[PIECE * low + v]
-    direct = decode(fields[0], fields[1])
-    high, low = split(jnp.concatenate(decode(fields[2], fields[3]), axis=1))
-    mirror = product(flip_rows[...], jnp.concatenate([high, low], axis=0))
     scale = f32(0.5 / (NX * NY))
-    top = lax.broadcasted_iota(jnp.int32, (DEVICES, LANES), 0) == 0
+    direct, mirror = decode(fields[0], fields[1]), decode(fields[2], fields[3])
     for f in range(4):
-        lines = jnp.concatenate(split(mirror[:, f * LANES : (f + 1) * LANES]), axis=1)
-        first = product(lines[0 : 2 * ROWS], flip_lams[1])
-        lines = product(lines, flip_lams[0])
-        lines = jnp.where(top, jnp.broadcast_to(first[0:1], lines.shape), lines)
-        response[f] = (direct[f] + lines if f % 2 == 0 else direct[f] - lines) * scale
+        response[f] = (direct[f] + mirror[f] if f % 2 == 0 else direct[f] - mirror[f]) * scale
 
 
 def exchange(sent, axis, count):
@@ -547,16 +561,23 @@
                 pltpu.SMEM((2,), jnp.int32),
             ]
             + [pltpu.VMEM(sky_image.shape, f32)] * 3
-            + [pltpu.SemaphoreType.DMA((5,))],
+            + [
+                pltpu.VMEM((SHORT, TILE_ROWS + 6 * ROWS, LANES), jnp.bfloat16),
+                pltpu.SemaphoreType.DMA((5,)),
+                pltpu.SemaphoreType.DMA((4,)),
+            ],
         ),
         "sx",
         SHORT,
     )
+    special = jnp.where(band * SHORT + column < PIECE, 1, 0).astype(jnp.int32).reshape(1)
     spread = run(
         pack_transfer,
         shaped(4, DEVICES, LANES, dtype=jnp.int32),
+        special,
         transfer,
         tables["flips"],
+        scalars=1,
         scratch=[pltpu.VMEM((8, DEVICES, LANES), f32)],
     )
     work = [pltpu.VMEM((DEVICES, 2 * LANES), f32)]
@@ -590,8 +611,6 @@
         middle_lines,
         [shaped(DEVICES, LANES, dtype=jnp.int32), shaped(4, DEVICES, LANES)],
         received,
-        tables["flip_rows"],
-        tables["flip_lams"],
         *y_tables,
         scratch=[pltpu.VMEM((4, DEVICES, LANES), jnp.int32)],
     )

time: 142 us -> 142 us (level)
  no operation moved by 1% of the time
where the time goes in v4:
time: 142 us; the launch traced here: 141 us
  blocking collectives  86.1 us (61%)
  waiting for transfers between devices  23.1 us (16%)
  starting transfers between devices  16.9 us (12%)
  Pallas kernels  12.7 us (9%)
    all_to_all x4, blocking collectives, exchange(): lax.all_to_all(sent.reshape(shape), axis, split_axis=0, concat_axis=0, ti...  86.1 us
    all_to_all x2, waiting for transfers between devices, exchange(): lax.all_to_all(sent.reshape(shape), axis, split_axis=0, concat_axis=0, ti...  20.4 us
    all_to_all x2, starting transfers between devices, exchange(): lax.all_to_all(sent.reshape(shape), axis, split_axis=0, concat_axis=0, ti...  14.5 us
    pallas_call x8, Pallas kernels, run(): pl.pallas_call(body, out_shape=shapes, in_specs=[pl.BlockSpec(memory_spac...  12.7 us
  transfers between devices with their start and end apart: 4, of which 4 were waited for; matrix products, arithmetic and copies ran while one was open for 1% of the time, Pallas kernels for 1%

profile of v4, /device:TPU:1, one launch (start us, length us, event | category | flops | bytes accessed | tf_op | source)
XLA Modules:
  0.0 141.4 jit_solution(8677256908888647351)
XLA Ops:
  0.6 2.0 %shard_map.158 = bf16[32,80,128]{2,1,0:T(8,128)(2,1)} custom-call(bf16[4,128,128]{2,1,0:T(8,128)(2,1)} %refs_0_.1, s32[2]{0:T(128)} %bitcast.25, f32[256,128]{1,0:T(8,128)} %refs_2_.1, f32[256,128]{1,0:T(8,128)} %refs_3_.1, f32[256,128]{1,0:T(8,128)} %refs_4_.1), custom_call_target="tpu_custom_call" | custom-call | tf_op jit(solution)/shard_map/pallas_call | solution.py:107
  2.6 8.7 %all-to-all-start = ((bf16[32,80,128]{2,1,0:T(8,128)(2,1)}), bf16[32,80,128]{2,1,0:T(8,128)(2,1)S(1)}, u32[]{:S(2)}, u32[]{:S(2)}) async-start(bf16[32,80,128]{2,1,0:T(8,128)(2,1)} %shard_map.158), calls=%async_computation | async-start | bytes 1310720 | tf_op jit(solution)/shard_map/all_to_all | solution.py:536
  11.4 0.7 dynamic-slice_subtract_fusion
  12.1 0.1 copy.19
  12.2 0.1 sub.15.wanted
  12.3 1.4 %shard_map.159.spread = s32[4,256,128]{2,1,0:T(8,128)S(1)} custom-call(s32[1]{0:T(128)} %bitcast.1.special, f32[4,2,8,4096]{3,2,1,0:T(8,128)S(1)} %copy-done.5, bf16[2,256,128]{2,1,0:T(8,128)(2,1)S(1)} %copy-done.8), custom_call_target="tpu_custom_call" | custom-call | tf_op jit(solution)/shard_map/pallas_call | solution.py:107
  13.8 10.5 %all-to-all-done.parts = bf16[32,80,128]{2,1,0:T(8,128)(2,1)S(1)} async-done(((bf16[32,80,128]{2,1,0:T(8,128)(2,1)}), bf16[32,80,128]{2,1,0:T(8,128)(2,1)S(1)}, u32[]{:S(2)}, u32[]{:S(2)}) %all-to-all-start) | async-done | bytes 655392 | tf_op jit(solution)/shard_map/all_to_all | solution.py:536
  24.3 1.6 %shard_map.160 = (s32[1536,128]{1,0:T(8,128)S(1)}, f32[4,32,8,128]{3,2,1,0:T(8,128)S(1)}, f32[32,8,128]{2,1,0:T(8,128)S(1)}, f32[32,128]{1,0:T(8,128)S(1)}, f32[32,128]{1,0:T(8,128)S(1)}) custom-call(s32[128]{0:T(128)S(1)} %sub.15.wanted, bf16[32,80,128]{2,1,0:T(8,128)(2,1)S(1)} %all-to-all-done.parts, s32[4,256,128]{2,1,0:T(8,128)S(1)} %shard_map.159.spread, ...), custom_call_target="tpu_custom_call" | custom-call | tf_op jit(solution)/shard_map/pallas_call | solution.py:107
  26.0 35.7 %all_to_all.30 = s32[256,1,768]{2,1,0:T(1,128)S(1)} all-to-all(s32[256,1,768]{2,1,0:T(1,128)S(1)} %bitcast.20), channel_id=1, replica_groups=mesh['sy'=8,'sx'=32] {'sy','sx'}, dimensions={0} | all-to-all | bytes 1572864 | tf_op jit(solution)/shard_map/all_to_all | solution.py:536
  61.7 2.4 %shard_map.161 = (s32[256,128]{1,0:T(8,128)S(1)}, f32[4,256,128]{2,1,0:T(8,128)S(1)}) custom-call(s32[1536,128]{1,0:T(8,128)S(1)} %bitcast.18, bf16[512,768]{1,0:T(8,128)(2,1)S(1)} %copy-done, f32[2,256,128]{2,1,0:T(8,128)S(1)} %copy-done.6, bf16[768,256]{1,0:T(8,128)(2,1)S(1)} %copy-done.2, bf16[768,256]{1,0:T(8,128)(2,1)S(1)} %copy-done.3), custom_call_target="tpu_custom_call" | custom-call | tf_op jit(solution)/shard_map/pallas_call | solution.py:107
  64.1 19.2 %all_to_all.31 = s32[256,1,128]{2,1,0:T(1,128)S(1)} all-to-all(s32[256,1,128]{2,1,0:T(1,128)S(1)} %bitcast.24), channel_id=1, replica_groups=mesh['sy'=8,'sx'=32] {'sy','sx'}, dimensions={0} | all-to-all | bytes 262144 | tf_op jit(solution)/shard_map/all_to_all | solution.py:536
  83.3 1.4 %shard_map.162 = (s32[256,128]{1,0:T(8,128)S(1)}, f32[32,8,128]{2,1,0:T(8,128)S(1)}) custom-call(s32[256,128]{1,0:T(8,128)S(1)} %bitcast.21, bf16[32,80,128]{2,1,0:T(8,128)(2,1)S(1)} %all-to-all-done.parts, f32[2,32,128]{2,1,0:T(8,128)S(1)} %copy-done.7, bf16[768,256]{1,0:T(8,128)(2,1)S(1)} %copy-done.4, bf16[768,256]{1,0:T(8,128)(2,1)S(1)} %copy-done.1), custom_call_target="tpu_custom_call" | custom-call | tf_op jit(solution)/shard_map/pallas_call | solution.py:107
  84.7 18.4 %all_to_all.32 = s32[256,1,128]{2,1,0:T(1,128)S(1)} all-to-all(s32[256,1,128]{2,1,0:T(1,128)S(1)} %bitcast.23), channel_id=1, replica_groups=mesh['sy'=8,'sx'=32] {'sy','sx'}, dimensions={0} | all-to-all | bytes 262144 | tf_op jit(solution)/shard_map/all_to_all | solution.py:536
  103.1 2.6 %shard_map.163 = s32[512,128]{1,0:T(8,128)} custom-call(s32[256,128]{1,0:T(8,128)S(1)} %bitcast.22, f32[4,256,128]{2,1,0:T(8,128)S(1)} %get-tuple-element.14.response, bf16[512,768]{1,0:T(8,128)(2,1)S(1)} %copy-done, f32[2,256,128]{2,1,0:T(8,128)S(1)} %copy-done.6, bf16[768,256]{1,0:T(8,128)(2,1)S(1)} %copy-done.2, bf16[768,256]{1,0:T(8,128)(2,1)S(1)} %copy-done.3), custom_call_target="tpu_custom_call" | custom-call | tf_op jit(solution)/shard_map/pallas_call | solution.py:107
  105.7 5.7 %all-to-all-start.4 = ((s32[256,2,128]{2,1,0:T(2,128)}), s32[256,2,128]{2,1,0:T(2,128)S(1)}, u32[]{:S(2)}, u32[]{:S(2)}) async-start(s32[256,2,128]{2,1,0:T(2,128)} %bitcast.10), calls=%async_computation.4 | async-start | bytes 524288 | tf_op jit(solution)/shard_map/all_to_all | solution.py:536
  111.4 1.7 %collective-permute-start = (f32[32,128]{1,0:T(8,128)S(1)}, f32[32,128]{1,0:T(8,128)S(1)}, u32[]{:S(2)}, u32[]{:S(2)}) collective-permute-start(f32[32,128]{1,0:T(8,128)S(1)} %get-tuple-element.18), channel_id=1, source_target_pairs={{0,1},{1,2},{2,3},{3,4},{4,5},{5,6},{6,7},{7,8},{8,9},{9,10},{10,1... | collective-permute-start | bytes 49160 | tf_op jit(solution)/shard_map/ppermute | solution.py:605
  113.2 0.7 collective-permute-start.1
  113.9 0.6 collective-permute-done.above
  114.5 2.2 %collective-permute-done.1.below = f32[32,128]{1,0:T(8,128)S(1)} collective-permute-done((f32[32,128]{1,0:T(8,128)S(1)}, f32[32,128]{1,0:T(8,128)S(1)}, u32[]{:S(2)}, u32[]{:S(2)}) %collective-permute-start.1) | collective-permute-done | bytes 16416 | tf_op jit(solution)/shard_map/ppermute | solution.py:606
  116.7 0.3 shard_map.164.flow
  116.9 9.9 %all-to-all-done.4 = s32[256,2,128]{2,1,0:T(2,128)S(1)} async-done(((s32[256,2,128]{2,1,0:T(2,128)}), s32[256,2,128]{2,1,0:T(2,128)S(1)}, u32[]{:S(2)}, u32[]{:S(2)}) %all-to-all-start.4) | async-done | bytes 262176 | tf_op jit(solution)/shard_map/all_to_all | solution.py:536
  126.8 0.9 shard_map.165
  127.8 12.9 %all_to_all.33 = f32[32,16,128]{2,1,0:T(8,128)S(1)} all-to-all(f32[32,16,128]{2,1,0:T(8,128)S(1)} %shard_map.165), channel_id=1, replica_groups=mesh['sy'=8,'sx'=32] {'sx'}, dimensions={0} | all-to-all | bytes 524288 | tf_op jit(solution)/shard_map/all_to_all | solution.py:536
  140.7 0.7 slice_bitcast_fusion
  (18 shorter events, 0.1 us)
Async XLA Ops:
  0.6 11.7 %copy-start.5 = (f32[4,2,8,4096]{3,2,1,0:T(8,128)S(1)}, f32[4,2,8,4096]{3,2,1,0:T(8,128)}, u32[]{:S(2)}) copy-start(f32[4,2,8,4096]{3,2,1,0:T(8,128)} %transfer.1) | copy-start | bytes 3145732
  2.6 9.7 %copy-start.8 = (bf16[2,256,128]{2,1,0:T(8,128)(2,1)S(1)}, bf16[2,256,128]{2,1,0:T(8,128)(2,1)}, u32[]{:S(2)}) copy-start(bf16[2,256,128]{2,1,0:T(8,128)(2,1)} %constant.57.clone.flips) | copy-start | bytes 393220
  2.6 21.6 %all-to-all-start = ((bf16[32,80,128]{2,1,0:T(8,128)(2,1)}), bf16[32,80,128]{2,1,0:T(8,128)(2,1)S(1)}, u32[]{:S(2)}, u32[]{:S(2)}) async-start(bf16[32,80,128]{2,1,0:T(8,128)(2,1)} %shard_map.158), calls=%async_computation | async-start | bytes 1310720 | tf_op jit(solution)/shard_map/all_to_all | solution.py:536
  12.3 12.0 %copy-start.4 = (bf16[768,256]{1,0:T(8,128)(2,1)S(1)}, bf16[768,256]{1,0:T(8,128)(2,1)}, u32[]{:S(2)}) copy-start(bf16[768,256]{1,0:T(8,128)(2,1)} %constant.51.clone.matrix.forward) | copy-start | bytes 1179652
  12.3 12.0 %copy-start.7 = (f32[2,32,128]{2,1,0:T(8,128)S(1)}, f32[2,32,128]{2,1,0:T(8,128)}, u32[]{:S(2)}) copy-start(f32[2,32,128]{2,1,0:T(8,128)} %constant.50.clone.turn) | copy-start | bytes 98308
  24.3 37.4 %copy-start.6 = (f32[2,256,128]{2,1,0:T(8,128)S(1)}, f32[2,256,128]{2,1,0:T(8,128)}, u32[]{:S(2)}) copy-start(f32[2,256,128]{2,1,0:T(8,128)} %constant.54.clone.turn_y) | copy-start | bytes 786436
  25.9 35.7 %copy-start = (bf16[512,768]{1,0:T(8,128)(2,1)S(1)}, bf16[512,768]{1,0:T(8,128)(2,1)}, u32[]{:S(2)}) copy-start(bf16[512,768]{1,0:T(8,128)(2,1)} %constant.53.clone.y_long) | copy-start | bytes 2359300
  26.0 35.7 %copy-start.2 = (bf16[768,256]{1,0:T(8,128)(2,1)S(1)}, bf16[768,256]{1,0:T(8,128)(2,1)}, u32[]{:S(2)}) copy-start(bf16[768,256]{1,0:T(8,128)(2,1)} %constant.55.clone.forward) | copy-start | bytes 1179652
  26.0 35.7 %copy-start.3 = (bf16[768,256]{1,0:T(8,128)(2,1)S(1)}, bf16[768,256]{1,0:T(8,128)(2,1)}, u32[]{:S(2)}) copy-start(bf16[768,256]{1,0:T(8,128)(2,1)} %constant.56.clone.inverse) | copy-start | bytes 1179652
  61.7 21.6 %copy-start.1 = (bf16[768,256]{1,0:T(8,128)(2,1)S(1)}, bf16[768,256]{1,0:T(8,128)(2,1)}, u32[]{:S(2)}) copy-start(bf16[768,256]{1,0:T(8,128)(2,1)} %constant.52.clone.inverse) | copy-start | bytes 1179652
  105.7 21.1 %all-to-all-start.4 = ((s32[256,2,128]{2,1,0:T(2,128)}), s32[256,2,128]{2,1,0:T(2,128)S(1)}, u32[]{:S(2)}, u32[]{:S(2)}) async-start(s32[256,2,128]{2,1,0:T(2,128)} %bitcast.10), calls=%async_computation.4 | async-start | bytes 524288 | tf_op jit(solution)/shard_map/all_to_all | solution.py:536
  111.4 3.0 %collective-permute-start = (f32[32,128]{1,0:T(8,128)S(1)}, f32[32,128]{1,0:T(8,128)S(1)}, u32[]{:S(2)}, u32[]{:S(2)}) collective-permute-start(f32[32,128]{1,0:T(8,128)S(1)} %get-tuple-element.18), channel_id=1, source_target_pairs={{0,1},{1,2},{2,3},{3,4},{4,5},{5,6},{6,7},{7,8},{8,9},{9,10},{10,1... | collective-permute-start | bytes 49160 | tf_op jit(solution)/shard_map/ppermute | solution.py:605
  113.2 3.5 %collective-permute-start.1 = (f32[32,128]{1,0:T(8,128)S(1)}, f32[32,128]{1,0:T(8,128)S(1)}, u32[]{:S(2)}, u32[]{:S(2)}) collective-permute-start(f32[32,128]{1,0:T(8,128)S(1)} %get-tuple-element.19), channel_id=1, source_target_pairs={{1,0},{2,1},{3,2},{4,3},{5,4},{6,5},{7,6},{8,7},{9,8},{10,9},{11,1... | collective-permute-start | bytes 49160 | tf_op jit(solution)/shard_map/ppermute | solution.py:606

commit v5 on v4

--- a/solution.py
+++ b/solution.py
@@ -382,8 +382,8 @@
                 pair.append(value * sky)
             points.append(tuple(pair))
         fields += rows_to_lines(points, turn, matrix, work)
+    sent[...] = spread[...]
     put(sent, [swapped(word) for word in encode(fields)], 0, 6)
-    put(sent, [spread[word] for word in range(4)], 2, 6)
 
 
 def middle_lines(received, y_long, turn_y, forward, inverse, sent, response, fields):
@@ -493,12 +493,12 @@
         blocks = [first[:ROWS]]
         blocks += [others[ROWS * c : ROWS * (c + 1)] for c in range(SHORT - 1, 0, -1)]
         reverse.append(jnp.concatenate(blocks, axis=0))
-    for w, word in enumerate(encode(direct)):
-        sent[w] = swapped(word)
+    put(sent, [jnp.zeros((DEVICES, LANES), jnp.int32)] * 2, 0, 6)
+    put(sent, [swapped(word) for word in encode(direct)], 2, 6)
     for w, word in enumerate(encode(reverse)):
         word = reversed_rows(word.reshape(SHORT, ROWS, LANES))
         word = jnp.where(special[0] == 1, pltpu.roll(word, 1, 1), word)
-        sent[2 + w] = swap_blocks(word).reshape(DEVICES, LANES)
+        put(sent, [swap_blocks(word).reshape(DEVICES, LANES)], 4 + w, 6)
 
 
 def mirrored_blocks(blocks):
@@ -573,7 +573,7 @@
     special = jnp.where(band * SHORT + column < PIECE, 1, 0).astype(jnp.int32).reshape(1)
     spread = run(
         pack_transfer,
-        shaped(4, DEVICES, LANES, dtype=jnp.int32),
+        shaped(DEVICES * 6, LANES, dtype=jnp.int32),
         special,
         transfer,
         tables["flips"],

time: 142 us -> 142 us (level)
  no operation moved by 1% of the time
where the time goes in v5:
time: 142 us; the launch traced here: 141 us
  blocking collectives  86.2 us (61%)
  waiting for transfers between devices  23.1 us (16%)
  starting transfers between devices  16.9 us (12%)
  Pallas kernels  12.7 us (9%)
    all_to_all x4, blocking collectives, exchange(): lax.all_to_all(sent.reshape(shape), axis, split_axis=0, concat_axis=0, ti...  86.2 us
    all_to_all x2, waiting for transfers between devices, exchange(): lax.all_to_all(sent.reshape(shape), axis, split_axis=0, concat_axis=0, ti...  20.4 us
    all_to_all x2, starting transfers between devices, exchange(): lax.all_to_all(sent.reshape(shape), axis, split_axis=0, concat_axis=0, ti...  14.4 us
    pallas_call x8, Pallas kernels, run(): pl.pallas_call(body, out_shape=shapes, in_specs=[pl.BlockSpec(memory_spac...  12.7 us
  transfers between devices with their start and end apart: 4, of which 4 were waited for; matrix products, arithmetic and copies ran while one was open for 1% of the time, Pallas kernels for 1%

profile of v5, /device:TPU:1, one launch (start us, length us, event | category | flops | bytes accessed | tf_op | source)
XLA Modules:
  0.0 141.4 jit_solution(11257564825945496253)
XLA Ops:
  0.6 2.0 %shard_map.158 = bf16[32,80,128]{2,1,0:T(8,128)(2,1)} custom-call(bf16[4,128,128]{2,1,0:T(8,128)(2,1)} %refs_0_.1, s32[2]{0:T(128)} %bitcast.25, f32[256,128]{1,0:T(8,128)} %refs_2_.1, f32[256,128]{1,0:T(8,128)} %refs_3_.1, f32[256,128]{1,0:T(8,128)} %refs_4_.1), custom_call_target="tpu_custom_call" | custom-call | tf_op jit(solution)/shard_map/pallas_call | solution.py:107
  2.6 8.7 %all-to-all-start = ((bf16[32,80,128]{2,1,0:T(8,128)(2,1)}), bf16[32,80,128]{2,1,0:T(8,128)(2,1)S(1)}, u32[]{:S(2)}, u32[]{:S(2)}) async-start(bf16[32,80,128]{2,1,0:T(8,128)(2,1)} %shard_map.158), calls=%async_computation | async-start | bytes 1310720 | tf_op jit(solution)/shard_map/all_to_all | solution.py:536
  11.4 0.7 dynamic-slice_subtract_fusion
  12.1 0.1 copy.19
  12.2 0.1 sub.15.wanted
  12.3 1.4 %shard_map.159.spread = s32[1536,128]{1,0:T(8,128)S(1)} custom-call(s32[1]{0:T(128)} %bitcast.1.special, f32[4,2,8,4096]{3,2,1,0:T(8,128)S(1)} %copy-done.5, bf16[2,256,128]{2,1,0:T(8,128)(2,1)S(1)} %copy-done.8), custom_call_target="tpu_custom_call" | custom-call | tf_op jit(solution)/shard_map/pallas_call | solution.py:107
  13.8 10.5 %all-to-all-done.parts = bf16[32,80,128]{2,1,0:T(8,128)(2,1)S(1)} async-done(((bf16[32,80,128]{2,1,0:T(8,128)(2,1)}), bf16[32,80,128]{2,1,0:T(8,128)(2,1)S(1)}, u32[]{:S(2)}, u32[]{:S(2)}) %all-to-all-start) | async-done | bytes 655392 | tf_op jit(solution)/shard_map/all_to_all | solution.py:536
  24.3 1.6 %shard_map.160 = (s32[1536,128]{1,0:T(8,128)S(1)}, f32[4,32,8,128]{3,2,1,0:T(8,128)S(1)}, f32[32,8,128]{2,1,0:T(8,128)S(1)}, f32[32,128]{1,0:T(8,128)S(1)}, f32[32,128]{1,0:T(8,128)S(1)}) custom-call(s32[128]{0:T(128)S(1)} %sub.15.wanted, bf16[32,80,128]{2,1,0:T(8,128)(2,1)S(1)} %all-to-all-done.parts, s32[1536,128]{1,0:T(8,128)S(1)} %shard_map.159.spread, ...), custom_call_target="tpu_custom_call" | custom-call | tf_op jit(solution)/shard_map/pallas_call | solution.py:107
  26.0 35.7 %all_to_all.30 = s32[256,1,768]{2,1,0:T(1,128)S(1)} all-to-all(s32[256,1,768]{2,1,0:T(1,128)S(1)} %bitcast.20), channel_id=1, replica_groups=mesh['sy'=8,'sx'=32] {'sy','sx'}, dimensions={0} | all-to-all | bytes 1572864 | tf_op jit(solution)/shard_map/all_to_all | solution.py:536
  61.7 2.4 %shard_map.161 = (s32[256,128]{1,0:T(8,128)S(1)}, f32[4,256,128]{2,1,0:T(8,128)S(1)}) custom-call(s32[1536,128]{1,0:T(8,128)S(1)} %bitcast.18, bf16[512,768]{1,0:T(8,128)(2,1)S(1)} %copy-done, f32[2,256,128]{2,1,0:T(8,128)S(1)} %copy-done.6, bf16[768,256]{1,0:T(8,128)(2,1)S(1)} %copy-done.2, bf16[768,256]{1,0:T(8,128)(2,1)S(1)} %copy-done.3), custom_call_target="tpu_custom_call" | custom-call | tf_op jit(solution)/shard_map/pallas_call | solution.py:107
  64.0 19.2 %all_to_all.31 = s32[256,1,128]{2,1,0:T(1,128)S(1)} all-to-all(s32[256,1,128]{2,1,0:T(1,128)S(1)} %bitcast.24), channel_id=1, replica_groups=mesh['sy'=8,'sx'=32] {'sy','sx'}, dimensions={0} | all-to-all | bytes 262144 | tf_op jit(solution)/shard_map/all_to_all | solution.py:536
  83.3 1.4 %shard_map.162 = (s32[256,128]{1,0:T(8,128)S(1)}, f32[32,8,128]{2,1,0:T(8,128)S(1)}) custom-call(s32[256,128]{1,0:T(8,128)S(1)} %bitcast.21, bf16[32,80,128]{2,1,0:T(8,128)(2,1)S(1)} %all-to-all-done.parts, f32[2,32,128]{2,1,0:T(8,128)S(1)} %copy-done.7, bf16[768,256]{1,0:T(8,128)(2,1)S(1)} %copy-done.4, bf16[768,256]{1,0:T(8,128)(2,1)S(1)} %copy-done.1), custom_call_target="tpu_custom_call" | custom-call | tf_op jit(solution)/shard_map/pallas_call | solution.py:107
  84.7 18.4 %all_to_all.32 = s32[256,1,128]{2,1,0:T(1,128)S(1)} all-to-all(s32[256,1,128]{2,1,0:T(1,128)S(1)} %bitcast.23), channel_id=1, replica_groups=mesh['sy'=8,'sx'=32] {'sy','sx'}, dimensions={0} | all-to-all | bytes 262144 | tf_op jit(solution)/shard_map/all_to_all | solution.py:536
  103.1 2.6 %shard_map.163 = s32[512,128]{1,0:T(8,128)} custom-call(s32[256,128]{1,0:T(8,128)S(1)} %bitcast.22, f32[4,256,128]{2,1,0:T(8,128)S(1)} %get-tuple-element.14.response, bf16[512,768]{1,0:T(8,128)(2,1)S(1)} %copy-done, f32[2,256,128]{2,1,0:T(8,128)S(1)} %copy-done.6, bf16[768,256]{1,0:T(8,128)(2,1)S(1)} %copy-done.2, bf16[768,256]{1,0:T(8,128)(2,1)S(1)} %copy-done.3), custom_call_target="tpu_custom_call" | custom-call | tf_op jit(solution)/shard_map/pallas_call | solution.py:107
  105.7 5.7 %all-to-all-start.4 = ((s32[256,2,128]{2,1,0:T(2,128)}), s32[256,2,128]{2,1,0:T(2,128)S(1)}, u32[]{:S(2)}, u32[]{:S(2)}) async-start(s32[256,2,128]{2,1,0:T(2,128)} %bitcast.10), calls=%async_computation.4 | async-start | bytes 524288 | tf_op jit(solution)/shard_map/all_to_all | solution.py:536
  111.4 1.7 %collective-permute-start = (f32[32,128]{1,0:T(8,128)S(1)}, f32[32,128]{1,0:T(8,128)S(1)}, u32[]{:S(2)}, u32[]{:S(2)}) collective-permute-start(f32[32,128]{1,0:T(8,128)S(1)} %get-tuple-element.18), channel_id=1, source_target_pairs={{0,1},{1,2},{2,3},{3,4},{4,5},{5,6},{6,7},{7,8},{8,9},{9,10},{10,1... | collective-permute-start | bytes 49160 | tf_op jit(solution)/shard_map/ppermute | solution.py:605
  113.1 0.7 collective-permute-start.1
  113.8 0.6 collective-permute-done.above
  114.4 2.2 %collective-permute-done.1.below = f32[32,128]{1,0:T(8,128)S(1)} collective-permute-done((f32[32,128]{1,0:T(8,128)S(1)}, f32[32,128]{1,0:T(8,128)S(1)}, u32[]{:S(2)}, u32[]{:S(2)}) %collective-permute-start.1) | collective-permute-done | bytes 16416 | tf_op jit(solution)/shard_map/ppermute | solution.py:606
  116.6 0.3 shard_map.164.flow
  116.9 9.9 %all-to-all-done.4 = s32[256,2,128]{2,1,0:T(2,128)S(1)} async-done(((s32[256,2,128]{2,1,0:T(2,128)}), s32[256,2,128]{2,1,0:T(2,128)S(1)}, u32[]{:S(2)}, u32[]{:S(2)}) %all-to-all-start.4) | async-done | bytes 262176 | tf_op jit(solution)/shard_map/all_to_all | solution.py:536
  126.8 0.9 shard_map.165
  127.7 12.9 %all_to_all.33 = f32[32,16,128]{2,1,0:T(8,128)S(1)} all-to-all(f32[32,16,128]{2,1,0:T(8,128)S(1)} %shard_map.165), channel_id=1, replica_groups=mesh['sy'=8,'sx'=32] {'sx'}, dimensions={0} | all-to-all | bytes 524288 | tf_op jit(solution)/shard_map/all_to_all | solution.py:536
  140.6 0.7 slice_bitcast_fusion
  (18 shorter events, 0.1 us)
Async XLA Ops:
  0.6 11.7 %copy-start.5 = (f32[4,2,8,4096]{3,2,1,0:T(8,128)S(1)}, f32[4,2,8,4096]{3,2,1,0:T(8,128)}, u32[]{:S(2)}) copy-start(f32[4,2,8,4096]{3,2,1,0:T(8,128)} %transfer.1) | copy-start | bytes 3145732
  2.6 9.7 %copy-start.8 = (bf16[2,256,128]{2,1,0:T(8,128)(2,1)S(1)}, bf16[2,256,128]{2,1,0:T(8,128)(2,1)}, u32[]{:S(2)}) copy-start(bf16[2,256,128]{2,1,0:T(8,128)(2,1)} %constant.57.clone.flips) | copy-start | bytes 393220
  2.6 21.6 %all-to-all-start = ((bf16[32,80,128]{2,1,0:T(8,128)(2,1)}), bf16[32,80,128]{2,1,0:T(8,128)(2,1)S(1)}, u32[]{:S(2)}, u32[]{:S(2)}) async-start(bf16[32,80,128]{2,1,0:T(8,128)(2,1)} %shard_map.158), calls=%async_computation | async-start | bytes 1310720 | tf_op jit(solution)/shard_map/all_to_all | solution.py:536
  12.3 12.0 %copy-start.4 = (bf16[768,256]{1,0:T(8,128)(2,1)S(1)}, bf16[768,256]{1,0:T(8,128)(2,1)}, u32[]{:S(2)}) copy-start(bf16[768,256]{1,0:T(8,128)(2,1)} %constant.51.clone.matrix.forward) | copy-start | bytes 1179652
  12.3 12.0 %copy-start.7 = (f32[2,32,128]{2,1,0:T(8,128)S(1)}, f32[2,32,128]{2,1,0:T(8,128)}, u32[]{:S(2)}) copy-start(f32[2,32,128]{2,1,0:T(8,128)} %constant.50.clone.turn) | copy-start | bytes 98308
  24.3 37.4 %copy-start.6 = (f32[2,256,128]{2,1,0:T(8,128)S(1)}, f32[2,256,128]{2,1,0:T(8,128)}, u32[]{:S(2)}) copy-start(f32[2,256,128]{2,1,0:T(8,128)} %constant.54.clone.turn_y) | copy-start | bytes 786436
  25.9 35.7 %copy-start = (bf16[512,768]{1,0:T(8,128)(2,1)S(1)}, bf16[512,768]{1,0:T(8,128)(2,1)}, u32[]{:S(2)}) copy-start(bf16[512,768]{1,0:T(8,128)(2,1)} %constant.53.clone.y_long) | copy-start | bytes 2359300
  25.9 35.7 %copy-start.2 = (bf16[768,256]{1,0:T(8,128)(2,1)S(1)}, bf16[768,256]{1,0:T(8,128)(2,1)}, u32[]{:S(2)}) copy-start(bf16[768,256]{1,0:T(8,128)(2,1)} %constant.55.clone.forward) | copy-start | bytes 1179652
  26.0 35.7 %copy-start.3 = (bf16[768,256]{1,0:T(8,128)(2,1)S(1)}, bf16[768,256]{1,0:T(8,128)(2,1)}, u32[]{:S(2)}) copy-start(bf16[768,256]{1,0:T(8,128)(2,1)} %constant.56.clone.inverse) | copy-start | bytes 1179652
  61.7 21.6 %copy-start.1 = (bf16[768,256]{1,0:T(8,128)(2,1)S(1)}, bf16[768,256]{1,0:T(8,128)(2,1)}, u32[]{:S(2)}) copy-start(bf16[768,256]{1,0:T(8,128)(2,1)} %constant.52.clone.inverse) | copy-start | bytes 1179652
  105.7 21.1 %all-to-all-start.4 = ((s32[256,2,128]{2,1,0:T(2,128)}), s32[256,2,128]{2,1,0:T(2,128)S(1)}, u32[]{:S(2)}, u32[]{:S(2)}) async-start(s32[256,2,128]{2,1,0:T(2,128)} %bitcast.10), calls=%async_computation.4 | async-start | bytes 524288 | tf_op jit(solution)/shard_map/all_to_all | solution.py:536
  111.4 3.0 %collective-permute-start = (f32[32,128]{1,0:T(8,128)S(1)}, f32[32,128]{1,0:T(8,128)S(1)}, u32[]{:S(2)}, u32[]{:S(2)}) collective-permute-start(f32[32,128]{1,0:T(8,128)S(1)} %get-tuple-element.18), channel_id=1, source_target_pairs={{0,1},{1,2},{2,3},{3,4},{4,5},{5,6},{6,7},{7,8},{8,9},{9,10},{10,1... | collective-permute-start | bytes 49160 | tf_op jit(solution)/shard_map/ppermute | solution.py:605
  113.1 3.5 %collective-permute-start.1 = (f32[32,128]{1,0:T(8,128)S(1)}, f32[32,128]{1,0:T(8,128)S(1)}, u32[]{:S(2)}, u32[]{:S(2)}) collective-permute-start(f32[32,128]{1,0:T(8,128)S(1)} %get-tuple-element.19), channel_id=1, source_target_pairs={{1,0},{2,1},{3,2},{4,3},{5,4},{6,5},{7,6},{8,7},{9,8},{10,9},{11,1... | collective-permute-start | bytes 49160 | tf_op jit(solution)/shard_map/ppermute | solution.py:606
